TPU v7x, 32 devices: a whole 2x2x4 slice. The times are simulated.
32 devices in a mesh: rep: 8 (over y, x, core), fsdp: 4 (over z).
Axes of the slice: x: 2, y: 2, z: 4, core: 2. Of those that a mesh axis runs over, the one named last changes fastest.
Arguments:
- tokens_in: bfloat16 [4096, 1024], P(('rep', 'fsdp')), may hold values from -20 to 20
- input_gain: float32 [1024], replicated, may hold values from 0.25 to 1.75
- q_gain: float32 [128], replicated, may hold values from 0.6 to 4.2
- k_gain: float32 [128], replicated, may hold values from 0.6 to 4.2
- w_query: bfloat16 [1024, 2048], P('fsdp'), may hold values from -0.35 to 0.35
- w_key: bfloat16 [1024, 1024], P('fsdp'), may hold values from -0.35 to 0.35
- w_value: bfloat16 [1024, 1024], P('fsdp'), may hold values from -0.1875 to 0.1875
- w_output: bfloat16 [2048, 1024], P('fsdp'), may hold values from -0.5 to 0.5
- post_gain: float32 [1024], replicated, may hold values from 0.25 to 1.75
- w_gate: bfloat16 [1024, 3072], P('fsdp'), may hold values from -0.1875 to 0.1875
- w_up: bfloat16 [1024, 3072], P('fsdp'), may hold values from -0.1875 to 0.1875
- w_down: bfloat16 [3072, 1024], P('fsdp'), may hold values from -0.109375 to 0.109375
- segment_ids: int32 [4096], P(('rep', 'fsdp')), may hold values from 0 to 95, as said below
- positions: int32 [4096], P(('rep', 'fsdp')), may hold values from 0 to 1926, as said below
- out_cotangent: bfloat16 [4096, 1024], P(('rep', 'fsdp')), may hold values from -19 to 19
Outputs:
- block_out: bfloat16 [4096, 1024], P(('rep', 'fsdp'))
- input_grad: bfloat16 [4096, 1024], P(('rep', 'fsdp'))
- grad_input_gain: float32 [1024], replicated
- grad_q_gain: float32 [128], replicated
- grad_k_gain: float32 [128], replicated
- grad_post_gain: float32 [1024], replicated
- grad_query: float32 [1024, 2048], P('fsdp')
- grad_key: float32 [1024, 1024], P('fsdp')
- grad_value: float32 [1024, 1024], P('fsdp')
- grad_output: float32 [2048, 1024], P('fsdp')
- grad_gate: float32 [1024, 3072], P('fsdp')
- grad_up: float32 [1024, 3072], P('fsdp')
- grad_down: float32 [3072, 1024], P('fsdp')
Inputs may be any that keep to these rules, and one draw needn't show every extreme that they name: `segment_ids`: each sequence of 128 tokens holds pieces of one to three documents; ids never fall along a sequence, no two sequences share an id, and ids may skip values. `positions`: positions rise by one from a token to the next of the same document and are 0 at a document's first token; the first document of a sequence may have begun in an earlier sequence.
All inputs are finite; a program needn't handle non-finite values.
Results may differ from a plain program's by a relative error of at most 0.017.
Values may be sent and summed in bfloat16 or wider, within the bound.
A program may use at most 192 MiB of HBM per device.

v0:
```python
from functools import partial
import math

import jax
import jax.numpy as jnp
from jax import lax
from jax.sharding import PartitionSpec as P

EPS = 1e-06
ROPE_BASE = 1000000.0
NEG_FILL = -1e30


def rms_scale(values):
    return lax.rsqrt(jnp.mean(values * values, axis=-1, keepdims=True) + EPS)


def rope_tables(places, width):
    halfway = width // 2
    ladder = jnp.arange(halfway, dtype=jnp.float32)
    inverse = jnp.exp(ladder * (-2.0 * math.log(ROPE_BASE) / width))
    angles = places.astype(jnp.float32)[:, None] * inverse[None, :]
    cosine = jnp.cos(angles)
    sine = jnp.sin(angles)
    return (
        jnp.concatenate([cosine, cosine], -1)[:, None, :],
        jnp.concatenate([sine, sine], -1)[:, None, :],
    )


def rotate(values):
    halfway = values.shape[-1] // 2
    return jnp.concatenate([-values[..., halfway:], values[..., :halfway]], -1)


def apply_rope(values, cosine, sine):
    return values * cosine + rotate(values) * sine


def undo_rope(grads, cosine, sine):
    return grads * cosine - rotate(grads * sine)


def norm_back(grads, values, scale, gain):
    normal = values * scale
    gain_term = jnp.sum(grads * normal, axis=tuple(range(grads.ndim - 1)))
    scaled = grads * gain
    back = scale * (scaled - normal * jnp.mean(scaled * normal, axis=-1, keepdims=True))
    return (back, gain_term)


def times_transposed(first, second):
    return lax.dot_general(
        first, second, (((1,), (1,)), ((), ())), preferred_element_type=jnp.float32
    )


def transposed_times(first, second):
    return lax.dot_general(
        first, second, (((0,), (0,)), ((), ())), preferred_element_type=jnp.float32
    )


def score_block(q_rot, k_rot, seg_ids, groups):
    length = q_rot.shape[0]
    heads_kv = k_rot.shape[1]
    width = k_rot.shape[2]
    grouped = q_rot.reshape(length, heads_kv, groups, width)
    scores = jnp.einsum(
        "qkgd,tkd->kgqt", grouped, k_rot, preferred_element_type=jnp.float32
    ) * width ** (-0.5)
    ladder = jnp.arange(length)
    allowed = (seg_ids[:, None] == seg_ids[None, :]) & (ladder[:, None] >= ladder[None, :])
    return (grouped, scores, allowed)


def attend_forward(q_rot, k_rot, values, seg_ids, groups):
    grouped, scores, allowed = score_block(q_rot, k_rot, seg_ids, groups)
    masked = jnp.where(allowed, scores, NEG_FILL)
    top = jnp.max(masked, axis=-1, keepdims=True)
    log_total = top + jnp.log(jnp.sum(jnp.exp(masked - top), axis=-1, keepdims=True))
    probs = jnp.where(allowed, jnp.exp(masked - log_total), 0.0).astype(jnp.bfloat16)
    mixed = jnp.einsum("kgqt,tkd->qkgd", probs, values, preferred_element_type=jnp.float32)
    return (mixed.reshape(q_rot.shape[0], -1).astype(jnp.bfloat16), log_total)


def attend_backward(q_rot, k_rot, values, seg_ids, log_total, d_mixed, groups):
    grouped, scores, allowed = score_block(q_rot, k_rot, seg_ids, groups)
    width = k_rot.shape[2]
    weights = jnp.where(allowed, jnp.exp(jnp.where(allowed, scores, NEG_FILL) - log_total), 0.0)
    d_grouped = d_mixed.reshape(grouped.shape)
    d_weights = jnp.einsum("qkgd,tkd->kgqt", d_grouped, values, preferred_element_type=jnp.float32)
    centre = jnp.sum(weights * d_weights, axis=-1, keepdims=True)
    d_scores = (weights * (d_weights - centre) * width ** (-0.5)).astype(jnp.bfloat16)
    d_query = jnp.einsum("kgqt,tkd->qkgd", d_scores, k_rot, preferred_element_type=jnp.float32)
    d_key = jnp.einsum("kgqt,qkgd->tkd", d_scores, grouped, preferred_element_type=jnp.float32)
    d_value = jnp.einsum(
        "kgqt,qkgd->tkd",
        weights.astype(jnp.bfloat16),
        d_grouped,
        preferred_element_type=jnp.float32,
    )
    return (d_query.reshape(q_rot.shape), d_key, d_value)


def layer_forward(
    tokens,
    seg_ids,
    places,
    input_gain,
    q_gain,
    k_gain,
    w_query,
    w_key,
    w_value,
    w_output,
    post_gain,
    w_gate,
    w_up,
    w_down,
    seq_len,
):
    rows_total = tokens.shape[0]
    width = q_gain.shape[0]
    seqs = rows_total // seq_len
    heads_q = w_query.shape[1] // width
    heads_kv = w_key.shape[1] // width
    groups = heads_q // heads_kv
    tokens_float = tokens.astype(jnp.float32)
    in_scale = rms_scale(tokens_float)
    normed = (tokens_float * in_scale * input_gain).astype(jnp.bfloat16)
    queries = jnp.dot(normed, w_query, preferred_element_type=jnp.float32).reshape(
        rows_total, heads_q, width
    )
    keys = jnp.dot(normed, w_key, preferred_element_type=jnp.float32).reshape(
        rows_total, heads_kv, width
    )
    values = (
        jnp.dot(normed, w_value, preferred_element_type=jnp.float32)
        .astype(jnp.bfloat16)
        .reshape(rows_total, heads_kv, width)
    )
    cosine, sine = rope_tables(places, width)
    q_scale = rms_scale(queries)
    k_scale = rms_scale(keys)
    q_rot = apply_rope(queries * q_scale * q_gain, cosine, sine).astype(jnp.bfloat16)
    k_rot = apply_rope(keys * k_scale * k_gain, cosine, sine).astype(jnp.bfloat16)
    attend = jax.vmap(partial(attend_forward, groups=groups))
    mixed, log_total = attend(
        q_rot.reshape(seqs, seq_len, heads_q, width),
        k_rot.reshape(seqs, seq_len, heads_kv, width),
        values.reshape(seqs, seq_len, heads_kv, width),
        seg_ids.reshape(seqs, seq_len),
    )
    attended = mixed.reshape(rows_total, heads_q * width)
    middle = tokens_float + jnp.dot(attended, w_output, preferred_element_type=jnp.float32)
    post_scale = rms_scale(middle)
    post_normed = (middle * post_scale * post_gain).astype(jnp.bfloat16)
    gate = jnp.dot(post_normed, w_gate, preferred_element_type=jnp.float32)
    up_proj = jnp.dot(post_normed, w_up, preferred_element_type=jnp.float32)
    hidden = (jax.nn.silu(gate) * up_proj).astype(jnp.bfloat16)
    block_out = (middle + jnp.dot(hidden, w_down, preferred_element_type=jnp.float32)).astype(
        jnp.bfloat16
    )
    saved = (
        tokens_float,
        in_scale,
        normed,
        queries,
        keys,
        q_scale,
        k_scale,
        values,
        q_rot,
        k_rot,
        cosine,
        sine,
        log_total,
        attended,
        middle,
        post_scale,
        post_normed,
        gate,
        up_proj,
        hidden,
    )
    return (block_out, saved)


def layer_backward(
    saved,
    seg_ids,
    cotangent,
    input_gain,
    q_gain,
    k_gain,
    w_query,
    w_key,
    w_value,
    w_output,
    post_gain,
    w_gate,
    w_up,
    w_down,
    seq_len,
):
    (
        tokens_float,
        in_scale,
        normed,
        queries,
        keys,
        q_scale,
        k_scale,
        values,
        q_rot,
        k_rot,
        cosine,
        sine,
        log_total,
        attended,
        middle,
        post_scale,
        post_normed,
        gate,
        up_proj,
        hidden,
    ) = saved
    rows_total = tokens_float.shape[0]
    width = q_gain.shape[0]
    seqs = rows_total // seq_len
    heads_q = queries.shape[1]
    heads_kv = keys.shape[1]
    groups = heads_q // heads_kv
    d_hidden = times_transposed(cotangent, w_down)
    sigm = jax.nn.sigmoid(gate)
    d_gate = (d_hidden * up_proj * sigm * (1.0 + gate * (1.0 - sigm))).astype(jnp.bfloat16)
    d_up = (d_hidden * gate * sigm).astype(jnp.bfloat16)
    d_post = times_transposed(d_gate, w_gate) + times_transposed(d_up, w_up)
    d_norm_mid, post_term = norm_back(d_post, middle, post_scale, post_gain)
    d_middle = cotangent.astype(jnp.float32) + d_norm_mid
    d_attn_out = d_middle.astype(jnp.bfloat16)
    d_attended = times_transposed(d_attn_out, w_output).astype(jnp.bfloat16)
    attend_back = jax.vmap(partial(attend_backward, groups=groups))
    d_qrot, d_krot, d_vals = attend_back(
        q_rot.reshape(seqs, seq_len, heads_q, width),
        k_rot.reshape(seqs, seq_len, heads_kv, width),
        values.reshape(seqs, seq_len, heads_kv, width),
        seg_ids.reshape(seqs, seq_len),
        log_total,
        d_attended.reshape(seqs, seq_len, heads_q * width),
    )
    q_back = undo_rope(d_qrot.reshape(rows_total, heads_q, width), cosine, sine)
    k_back = undo_rope(d_krot.reshape(rows_total, heads_kv, width), cosine, sine)
    d_q_float, q_term = norm_back(q_back, queries, q_scale, q_gain)
    d_k_float, k_term = norm_back(k_back, keys, k_scale, k_gain)
    d_queries = d_q_float.astype(jnp.bfloat16).reshape(rows_total, heads_q * width)
    d_keys = d_k_float.astype(jnp.bfloat16).reshape(rows_total, heads_kv * width)
    d_values = d_vals.astype(jnp.bfloat16).reshape(rows_total, heads_kv * width)
    d_normed = (
        times_transposed(d_queries, w_query)
        + times_transposed(d_keys, w_key)
        + times_transposed(d_values, w_value)
    )
    d_tokens, in_term = norm_back(d_normed, tokens_float, in_scale, input_gain)
    input_grad = (d_middle + d_tokens).astype(jnp.bfloat16)
    gains = (in_term, q_term, k_term, post_term)
    pairs = (
        (normed, d_queries),
        (normed, d_keys),
        (normed, d_values),
        (attended, d_attn_out),
        (post_normed, d_gate),
        (post_normed, d_up),
        (hidden, cotangent),
    )
    return (input_grad, gains, pairs)


def body(
    tokens_in,
    input_gain,
    q_gain,
    k_gain,
    w_query,
    w_key,
    w_value,
    w_output,
    post_gain,
    w_gate,
    w_up,
    w_down,
    segment_ids,
    positions,
    out_cotangent,
):
    seq_len = tokens_in.shape[0]
    attn_full = (
        lax.all_gather(w_query, "fsdp", axis=0, tiled=True),
        lax.all_gather(w_key, "fsdp", axis=0, tiled=True),
        lax.all_gather(w_value, "fsdp", axis=0, tiled=True),
        lax.all_gather(w_output, "fsdp", axis=0, tiled=True),
    )
    ffn_full = (
        lax.all_gather(w_gate, "fsdp", axis=0, tiled=True),
        lax.all_gather(w_up, "fsdp", axis=0, tiled=True),
        lax.all_gather(w_down, "fsdp", axis=0, tiled=True),
    )
    block_out, saved = layer_forward(
        tokens_in,
        segment_ids,
        positions,
        input_gain,
        q_gain,
        k_gain,
        attn_full[0],
        attn_full[1],
        attn_full[2],
        attn_full[3],
        post_gain,
        ffn_full[0],
        ffn_full[1],
        ffn_full[2],
        seq_len,
    )
    input_grad, gains, pairs = layer_backward(
        saved,
        segment_ids,
        out_cotangent,
        input_gain,
        q_gain,
        k_gain,
        attn_full[0],
        attn_full[1],
        attn_full[2],
        attn_full[3],
        post_gain,
        ffn_full[0],
        ffn_full[1],
        ffn_full[2],
        seq_len,
    )
    gain_total = lax.psum((gains[0], gains[1], gains[2], gains[3]), ("rep", "fsdp"))
    lefts = (
        lax.all_to_all(pairs[0][0], "fsdp", split_axis=1, concat_axis=0, tiled=True),
        lax.all_to_all(pairs[3][0], "fsdp", split_axis=1, concat_axis=0, tiled=True),
        lax.all_to_all(pairs[4][0], "fsdp", split_axis=1, concat_axis=0, tiled=True),
        lax.all_to_all(pairs[6][0], "fsdp", split_axis=1, concat_axis=0, tiled=True),
    )
    rights = (
        lax.all_gather(pairs[0][1], "fsdp", axis=0, tiled=True),
        lax.all_gather(pairs[1][1], "fsdp", axis=0, tiled=True),
        lax.all_gather(pairs[2][1], "fsdp", axis=0, tiled=True),
        lax.all_gather(pairs[3][1], "fsdp", axis=0, tiled=True),
        lax.all_gather(pairs[4][1], "fsdp", axis=0, tiled=True),
        lax.all_gather(pairs[5][1], "fsdp", axis=0, tiled=True),
        lax.all_gather(pairs[6][1], "fsdp", axis=0, tiled=True),
    )
    owned = (
        transposed_times(lefts[0], rights[0]),
        transposed_times(lefts[0], rights[1]),
        transposed_times(lefts[0], rights[2]),
        transposed_times(lefts[1], rights[3]),
        transposed_times(lefts[2], rights[4]),
        transposed_times(lefts[2], rights[5]),
        transposed_times(lefts[3], rights[6]),
    )
    grads = (
        lax.psum(owned[0].astype(jnp.bfloat16), "rep").astype(jnp.float32),
        lax.psum(owned[1].astype(jnp.bfloat16), "rep").astype(jnp.float32),
        lax.psum(owned[2].astype(jnp.bfloat16), "rep").astype(jnp.float32),
        lax.psum(owned[3].astype(jnp.bfloat16), "rep").astype(jnp.float32),
        lax.psum(owned[4].astype(jnp.bfloat16), "rep").astype(jnp.float32),
        lax.psum(owned[5].astype(jnp.bfloat16), "rep").astype(jnp.float32),
        lax.psum(owned[6].astype(jnp.bfloat16), "rep").astype(jnp.float32),
    )
    return (
        block_out,
        input_grad,
        gain_total[0],
        gain_total[1],
        gain_total[2],
        gain_total[3],
        grads[0],
        grads[1],
        grads[2],
        grads[3],
        grads[4],
        grads[5],
        grads[6],
    )


def solution(mesh):
    in_specs = (
        P(("rep", "fsdp"), None),
        P(),
        P(),
        P(),
        P("fsdp", None),
        P("fsdp", None),
        P("fsdp", None),
        P("fsdp", None),
        P(),
        P("fsdp", None),
        P("fsdp", None),
        P("fsdp", None),
        P(("rep", "fsdp")),
        P(("rep", "fsdp")),
        P(("rep", "fsdp"), None),
    )
    out_specs = (
        P(("rep", "fsdp"), None),
        P(("rep", "fsdp"), None),
        P(),
        P(),
        P(),
        P(),
        P("fsdp", None),
        P("fsdp", None),
        P("fsdp", None),
        P("fsdp", None),
        P("fsdp", None),
        P("fsdp", None),
        P("fsdp", None),
    )
    return jax.shard_map(body, mesh=mesh, in_specs=in_specs, out_specs=out_specs, check_vma=False)
```

profile of v0, /device:TPU:0, one launch (start us, length us, event | category | flops | bytes accessed | tf_op | source)
XLA Modules:
  0.0 1085.3 jit_solution(16811339082981558002)
XLA Ops:
  15.0 42.9 %all-gather.17.cloned.1.call-done = bf16[1024,1024]{1,0:T(8,128)(2,1)} async-done(((bf16[256,1024]{1,0:T(8,128)(2,1)}), bf16[1024,1024]{1,0:T(8,128)(2,1)}) %all-gather.17.cloned.1.call-update) | async-done | bytes 2097168 | tf_op jit(solution)/shard_map/all_gather | solution.py:300
  61.3 42.8 %all-gather.15.cloned.1.call-done = bf16[1024,1024]{1,0:T(8,128)(2,1)} async-done(((bf16[256,1024]{1,0:T(8,128)(2,1)}), bf16[1024,1024]{1,0:T(8,128)(2,1)}) %all-gather.15.cloned.1.call-update) | async-done | bytes 2097168 | tf_op jit(solution)/shard_map/all_gather | solution.py:301
  108.8 76.4 %all-gather.19.cloned.1.call-done = bf16[1024,2048]{1,0:T(8,128)(2,1)} async-done(((bf16[256,2048]{1,0:T(8,128)(2,1)}), bf16[1024,2048]{1,0:T(8,128)(2,1)}) %all-gather.19.cloned.1.call-update) | async-done | bytes 4194320 | tf_op jit(solution)/shard_map/all_gather | solution.py:299
  192.4 73.5 %all-gather.21.cloned.1.call-done = bf16[2048,1024]{1,0:T(8,128)(2,1)} async-done(((bf16[512,1024]{1,0:T(8,128)(2,1)}), bf16[2048,1024]{1,0:T(8,128)(2,1)}) %all-gather.21.cloned.1.call-update) | async-done | bytes 4194320 | tf_op jit(solution)/shard_map/all_gather | solution.py:302
  265.9 3.2 multiply_reduce_fusion.8
  269.7 111.4 %all-gather.23.cloned.1.call-done = bf16[1024,3072]{1,0:T(8,128)(2,1)} async-done(((bf16[256,3072]{1,0:T(8,128)(2,1)}), bf16[1024,3072]{1,0:T(8,128)(2,1)}) %all-gather.23.cloned.1.call-update) | async-done | bytes 6291472 | tf_op jit(solution)/shard_map/all_gather | solution.py:305
  381.1 4.9 fusion.45
  386.1 110.1 %all-gather.25.cloned.1.call-done = bf16[1024,3072]{1,0:T(8,128)(2,1)} async-done(((bf16[256,3072]{1,0:T(8,128)(2,1)}), bf16[1024,3072]{1,0:T(8,128)(2,1)}) %all-gather.25.cloned.1.call-update) | async-done | bytes 6291472 | tf_op jit(solution)/shard_map/all_gather | solution.py:306
  496.1 4.9 fusion.46
  501.0 110.2 %all-gather.27.cloned.1.call-done = bf16[3072,1024]{1,0:T(8,128)(2,1)} async-done(((bf16[768,1024]{1,0:T(8,128)(2,1)}), bf16[3072,1024]{1,0:T(8,128)(2,1)}) %all-gather.27.cloned.1.call-update) | async-done | bytes 6291472 | tf_op jit(solution)/shard_map/all_gather | solution.py:307
  611.2 7.7 multiply_convert_fusion
  618.9 6.1 fusion.47
  624.9 6.3 multiply_reduce_fusion.4
  632.9 4.6 convolution_convert_fusion.3
  683.6 3.4 all-to-all-start
  688.0 14.6 %all-to-all-done = bf16[128,4,256]{2,0,1:T(8,128)(2,1)S(1)} async-done(((bf16[128,4,256]{2,0,1:T(8,128)(2,1)}), bf16[128,4,256]{2,0,1:T(8,128)(2,1)S(1)}, u32[]{:S(2)}, u32[]{:S(2)}) %all-to-all-start) | async-done | bytes 262176 | tf_op jit(solution)/shard_map/all_to_all | solution.py:345
  702.6 4.2 all-to-all-start.3
  707.8 22.3 %all-to-all-done.3 = bf16[128,4,768]{2,0,1:T(8,128)(2,1)S(1)} async-done(((bf16[128,4,768]{2,0,1:T(8,128)(2,1)}), bf16[128,4,768]{2,0,1:T(8,128)(2,1)S(1)}, u32[]{:S(2)}, u32[]{:S(2)}) %all-to-all-start.3) | async-done | bytes 786464 | tf_op jit(solution)/shard_map/all_to_all | solution.py:348
  730.1 3.5 all-to-all-start.1
  734.3 3.4 convolution_convert_fusion.4
  740.2 20.7 %all-to-all-done.1 = bf16[128,4,512]{2,0,1:T(8,128)(2,1)S(1)} async-done(((bf16[128,4,512]{2,0,1:T(8,128)(2,1)}), bf16[128,4,512]{2,0,1:T(8,128)(2,1)S(1)}, u32[]{:S(2)}, u32[]{:S(2)}) %all-to-all-start.1) | async-done | bytes 524320 | tf_op jit(solution)/shard_map/all_to_all | solution.py:346
  760.8 3.4 all-to-all-start.2
  770.0 41.0 %all-gather.29.cloned.1.call-done = bf16[512,2048]{1,0:T(8,128)(2,1)} async-done(((bf16[128,2048]{1,0:T(8,128)(2,1)}), bf16[512,2048]{1,0:T(8,128)(2,1)}) %all-gather.29.cloned.1.call-update) | async-done | bytes 2097168 | tf_op jit(solution)/shard_map/all_gather | solution.py:351
  811.1 3.3 convolution_convert_fusion.2
  814.3 61.1 %all-gather.39.cloned.1.call-done = bf16[512,3072]{1,0:T(8,128)(2,1)} async-done(((bf16[128,3072]{1,0:T(8,128)(2,1)}), bf16[512,3072]{1,0:T(8,128)(2,1)}) %all-gather.39.cloned.1.call-update) | async-done | bytes 3145744 | tf_op jit(solution)/shard_map/all_gather | solution.py:356
  875.5 4.0 convolution_convert_fusion
  879.5 60.1 %all-gather.37.cloned.1.call-done = bf16[512,3072]{1,0:T(8,128)(2,1)} async-done(((bf16[128,3072]{1,0:T(8,128)(2,1)}), bf16[512,3072]{1,0:T(8,128)(2,1)}) %all-gather.37.cloned.1.call-update) | async-done | bytes 3145744 | tf_op jit(solution)/shard_map/all_gather | solution.py:355
  939.6 4.0 convolution_convert_fusion.1
  950.2 39.8 %all-reduce = (f32[1024]{0:T(1024)}, f32[128]{0:T(128)}, f32[128]{0:T(128)}, f32[1024]{0:T(1024)}) all-reduce(f32[1024]{0:T(1024)S(1)} %get-tuple-element.19, f32[128]{0:T(128)S(1)} %get-tuple-element.13, f32[128]{0:T(128)S(1)} %copy-done.65, f32[1024]{0:T(1024)S(1)} %copy-done.50), channel_id=1, replica_groups=mesh['rep'=8,'fsdp'=4] {'rep','fsdp'}, use_global_device_ids=true, to_apply=%region_12.13 | all-reduce | flops 2304 | bytes 18432 | tf_op jit(solution)/shard_map/psum | solution.py:343
  991.0 4.5 fusion.3
  995.5 70.3 %all-reduce.4.cloned.1.call-done = (bf16[256,2048]{1,0:T(8,128)(2,1)}, bf16[256,1024]{1,0:T(8,128)(2,1)}, bf16[256,1024]{1,0:T(8,128)(2,1)}, bf16[512,1024]{1,0:...) async-done(((bf16[256,2048]{1,0:T(8,128)(2,1)}, bf16[256,1024]{1,0:T(8,128)(2,1)}, bf16[256,1024]{1,0:T(8,128)(2,1)}, ...) | async-done | bytes 7864336 | tf_op jit(solution)/shard_map/psum | solution.py:369
  1065.8 3.6 convert_element_type.174
  (258 shorter events, 98.5 us)
Async XLA Ops:
  7.2 50.8 %all-gather.17.cloned.1.call-start = ((), (), s32[]{:S(2)}) async-start(), calls=%async_computation.5 | async-start | bytes 2621440 | tf_op jit(solution)/shard_map/all_gather | solution.py:300
  7.9 96.1 %all-gather.15.cloned.1.call-start = ((), (), s32[]{:S(2)}) async-start(), calls=%async_computation.4 | async-start | bytes 2621440 | tf_op jit(solution)/shard_map/all_gather | solution.py:301
  8.7 176.5 %all-gather.19.cloned.1.call-start = ((), (), s32[]{:S(2)}) async-start(), calls=%async_computation.6 | async-start | bytes 5242880 | tf_op jit(solution)/shard_map/all_gather | solution.py:299
  9.4 256.5 %all-gather.21.cloned.1.call-start = ((), (), s32[]{:S(2)}) async-start(), calls=%async_computation.7 | async-start | bytes 5242880 | tf_op jit(solution)/shard_map/all_gather | solution.py:302
  10.0 371.2 %all-gather.23.cloned.1.call-start = ((), (), s32[]{:S(2)}) async-start(), calls=%async_computation.8 | async-start | bytes 7864320 | tf_op jit(solution)/shard_map/all_gather | solution.py:305
  10.6 485.5 %all-gather.25.cloned.1.call-start = ((), (), s32[]{:S(2)}) async-start(), calls=%async_computation.9 | async-start | bytes 7864320 | tf_op jit(solution)/shard_map/all_gather | solution.py:306
  11.2 600.0 %all-gather.27.cloned.1.call-start = ((), (), s32[]{:S(2)}) async-start(), calls=%async_computation.10 | async-start | bytes 7864320 | tf_op jit(solution)/shard_map/all_gather | solution.py:307
  11.9 722.3 %all-gather.41.cloned.1.call-start = ((), (), s32[]{:S(2)}) async-start(), calls=%async_computation.17 | async-start | bytes 1310720 | tf_op jit(solution)/shard_map/all_gather | solution.py:357
  12.7 725.0 %all-gather.31.cloned.1.call-start = ((), (), s32[]{:S(2)}) async-start(), calls=%async_computation.12 | async-start | bytes 1310720 | tf_op jit(solution)/shard_map/all_gather | solution.py:352
  12.9 47.1 %copy-start.60 = (f32[128]{0:T(128)}, f32[128]{0:T(128)S(1)}, u32[]{:S(2)}) copy-start(f32[128]{0:T(128)S(1)} %add_rsqrt_fusion.3) | copy-start | bytes 1540
  15.0 170.2 %copy-start.8 = (bf16[128,1024]{1,0:T(8,128)(2,1)}, bf16[128,1024]{1,0:T(8,128)(2,1)S(1)}, u32[]{:S(2)}) copy-start(bf16[128,1024]{1,0:T(8,128)(2,1)S(1)} %fusion.18) | copy-start | bytes 786436
  61.3 46.6 %copy-start.55 = (f32[128]{0:T(128)S(1)}, f32[128]{0:T(128)}, u32[]{:S(2)}) copy-start(f32[128]{0:T(128)} %param.18) | copy-start | bytes 1540
  624.9 7.1 copy-start.45
  624.9 7.1 copy-start.58
  643.6 7.1 copy-start.16
  653.4 111.2 %all-gather.35.cloned.1.call-start = ((), (), s32[]{:S(2)}) async-start(), calls=%async_computation.14 | async-start | bytes 1310720 | tf_op jit(solution)/shard_map/all_gather | solution.py:354
  654.0 113.5 %all-gather.33.cloned.1.call-start = ((), (), s32[]{:S(2)}) async-start(), calls=%async_computation.13 | async-start | bytes 1310720 | tf_op jit(solution)/shard_map/all_gather | solution.py:353
  667.2 143.9 %all-gather.29.cloned.1.call-start = ((), (), s32[]{:S(2)}) async-start(), calls=%async_computation.11 | async-start | bytes 2621440 | tf_op jit(solution)/shard_map/all_gather | solution.py:351
  681.6 193.9 %all-gather.39.cloned.1.call-start = ((), (), s32[]{:S(2)}) async-start(), calls=%async_computation.16 | async-start | bytes 3932160 | tf_op jit(solution)/shard_map/all_gather | solution.py:356
  682.3 257.3 %all-gather.37.cloned.1.call-start = ((), (), s32[]{:S(2)}) async-start(), calls=%async_computation.15 | async-start | bytes 3932160 | tf_op jit(solution)/shard_map/all_gather | solution.py:355
  682.9 23.9 %copy-start.14 = (bf16[8,128,2,128]{3,1,2,0:T(8,128)(2,1)S(1)}, bf16[8,128,2,128]{3,1,2,0:T(8,128)(2,1)}, u32[]{:S(2)}) copy-start(bf16[8,128,2,128]{3,1,2,0:T(8,128)(2,1)} %convolution_convert_fusion.8) | copy-start | bytes 1572868
  683.6 19.0 %all-to-all-start = ((bf16[128,4,256]{2,0,1:T(8,128)(2,1)}), bf16[128,4,256]{2,0,1:T(8,128)(2,1)S(1)}, u32[]{:S(2)}, u32[]{:S(2)}) async-start(bf16[128,4,256]{2,0,1:T(8,128)(2,1)} %bitcast.202), calls=%async_computation | async-start | bytes 524288 | tf_op jit(solution)/shard_map/all_to_all | solution.py:345
  702.6 27.5 %all-to-all-start.3 = ((bf16[128,4,768]{2,0,1:T(8,128)(2,1)}), bf16[128,4,768]{2,0,1:T(8,128)(2,1)S(1)}, u32[]{:S(2)}, u32[]{:S(2)}) async-start(bf16[128,4,768]{2,0,1:T(8,128)(2,1)} %bitcast.200), calls=%async_computation.3 | async-start | bytes 1572864 | tf_op jit(solution)/shard_map/all_to_all | solution.py:348
  730.1 30.8 %all-to-all-start.1 = ((bf16[128,4,512]{2,0,1:T(8,128)(2,1)}), bf16[128,4,512]{2,0,1:T(8,128)(2,1)S(1)}, u32[]{:S(2)}, u32[]{:S(2)}) async-start(bf16[128,4,512]{2,0,1:T(8,128)(2,1)} %copy.183), calls=%async_computation.1 | async-start | bytes 1048576 | tf_op jit(solution)/shard_map/all_to_all | solution.py:346
  760.8 53.5 %all-to-all-start.2 = ((bf16[128,4,256]{2,0,1:T(8,128)(2,1)}), bf16[128,4,256]{2,0,1:T(8,128)(2,1)S(1)}, u32[]{:S(2)}, u32[]{:S(2)}) async-start(bf16[128,4,256]{2,0,1:T(8,128)(2,1)} %bitcast.201), calls=%async_computation.2 | async-start | bytes 524288 | tf_op jit(solution)/shard_map/all_to_all | solution.py:347
  764.3 301.6 %all-reduce.4.cloned.1.call-start = ((), (), s32[]{:S(2)}) async-start(), calls=%async_computation.18 | async-start | bytes 15728640 | tf_op jit(solution)/shard_map/psum | solution.py:369
  948.4 41.5 %copy-start.20 = (f32[128,1024]{1,0:T(8,128)S(1)}, f32[128,1024]{1,0:T(8,128)}, u32[]{:S(2)}) copy-start(f32[128,1024]{1,0:T(8,128)} %copy-done.19) | copy-start | bytes 1572868
  948.4 41.5 %copy-start.29 = (bf16[128,1024]{1,0:T(8,128)(2,1)S(1)}, bf16[128,1024]{1,0:T(8,128)(2,1)}, u32[]{:S(2)}) copy-start(bf16[128,1024]{1,0:T(8,128)(2,1)} %param.29) | copy-start | bytes 786436
  948.4 41.5 %copy-start.46 = (f32[1024]{0:T(1024)S(1)}, f32[1024]{0:T(1024)}, u32[]{:S(2)}) copy-start(f32[1024]{0:T(1024)} %param.23) | copy-start | bytes 12292
  948.4 41.5 %copy-start.59 = (f32[128]{0:T(128)S(1)}, f32[128]{0:T(128)}, u32[]{:S(2)}) copy-start(f32[128]{0:T(128)} %copy-done.57) | copy-start | bytes 1540
  948.5 41.5 %copy-start.64 = (f32[128]{0:T(128)S(1)}, f32[128]{0:T(128)}, u32[]{:S(2)}) copy-start(f32[128]{0:T(128)} %copy-done.63) | copy-start | bytes 1540
  950.2 40.8 %copy-start.24 = (bf16[128,3072]{1,0:T(8,128)(2,1)S(1)}, bf16[128,3072]{1,0:T(8,128)(2,1)}, u32[]{:S(2)}) copy-start(bf16[128,3072]{1,0:T(8,128)(2,1)} %get-tuple-element.34) | copy-start | bytes 2359300
  (54 other events, 115.2 us)
Sparse Core Ops, SparseCore 0:
  9.6 48.3 all-gather.16
  59.5 44.4 all-gather.14
  105.6 79.5 all-gather.18
  186.6 79.2 all-gather.20
  267.3 113.8 all-gather.22
  382.6 113.5 all-gather.24
  497.7 113.5 all-gather.26
  612.8 26.1 all-gather.40
  653.5 26.4 all-gather.30
  681.4 40.5 all-gather.34
  724.1 39.2 all-gather.32
  764.8 46.2 all-gather.28
  813.2 62.2 all-gather.38
  877.5 62.0 all-gather.36
  944.8 121.0 all-reduce.3
where the time goes:
time: 1090 us
  waiting for transfers between devices  864 us (79%)
  matrix products  84.4 us (8%)
  blocking collectives  39.8 us (4%)
  local copies, waits for them, and re-layouts  35.9 us (3%)
  other arithmetic  30.9 us (3%)
  starting transfers between devices  15.2 us (1%)
  between operations  14.7 us (1%)
    all_gather x1, waiting for transfers between devices, body(): lax.all_gather(w_gate, 'fsdp', axis=0, tiled=True)  111 us
    all_gather x1, waiting for transfers between devices, body(): lax.all_gather(w_down, 'fsdp', axis=0, tiled=True)  110 us
    all_gather x1, waiting for transfers between devices, body(): lax.all_gather(w_up, 'fsdp', axis=0, tiled=True)  110 us
    all_gather x1, waiting for transfers between devices, body(): lax.all_gather(w_query, 'fsdp', axis=0, tiled=True)  76.4 us
    all_gather x1, waiting for transfers between devices, body(): lax.all_gather(w_output, 'fsdp', axis=0, tiled=True)  73.5 us
    psum x1, waiting for transfers between devices, body(): lax.psum(owned[0].astype(jnp.bfloat16), 'rep').astype(jnp.float32)  70.3 us
    all_gather x1, waiting for transfers between devices, body(): lax.all_gather(pairs[5][1], 'fsdp', axis=0, tiled=True)  61.1 us
    all_gather x1, waiting for transfers between devices, body(): lax.all_gather(pairs[4][1], 'fsdp', axis=0, tiled=True)  60.1 us
  transfers between devices with their start and end apart: 19, of which 14 were waited for; matrix products, arithmetic and copies ran while one was open for 12% of the time, Pallas kernels for 0%

commit v1 on v0

--- a/solution.py
+++ b/solution.py
@@ -277,6 +277,35 @@
     return (input_grad, gains, pairs)
 
 
+def own_piece(shard):
+    rows = shard.shape[0] // lax.axis_size("rep")
+    return lax.dynamic_slice_in_dim(shard, lax.axis_index("rep") * rows, rows, 0)
+
+
+def gather_whole(shard):
+    return lax.all_gather(own_piece(shard), ("fsdp", "rep"), axis=0, tiled=True)
+
+
+def gather_staged(shard):
+    part = lax.all_gather(own_piece(shard), "fsdp", axis=0)
+    full = lax.all_gather(part, "rep", axis=1)
+    return full.reshape(-1, shard.shape[1])
+
+
+def sum_grad(first, second):
+    local = transposed_times(first, second).astype(jnp.bfloat16)
+    piece = lax.psum_scatter(local, ("fsdp", "rep"), scatter_dimension=0, tiled=True)
+    return lax.all_gather(piece, "rep", axis=0, tiled=True).astype(jnp.float32)
+
+
+def sum_gains(gains):
+    sizes = [gain.shape[0] for gain in gains]
+    packed = jnp.concatenate(gains)
+    total = jnp.sum(lax.all_gather(packed, ("fsdp", "rep"), axis=0), axis=0)
+    cuts = [sum(sizes[:at]) for at in range(1, len(sizes))]
+    return jnp.split(total, cuts)
+
+
 def body(
     tokens_in,
     input_gain,
@@ -296,16 +325,12 @@
 ):
     seq_len = tokens_in.shape[0]
     attn_full = (
-        lax.all_gather(w_query, "fsdp", axis=0, tiled=True),
-        lax.all_gather(w_key, "fsdp", axis=0, tiled=True),
-        lax.all_gather(w_value, "fsdp", axis=0, tiled=True),
-        lax.all_gather(w_output, "fsdp", axis=0, tiled=True),
-    )
-    ffn_full = (
-        lax.all_gather(w_gate, "fsdp", axis=0, tiled=True),
-        lax.all_gather(w_up, "fsdp", axis=0, tiled=True),
-        lax.all_gather(w_down, "fsdp", axis=0, tiled=True),
-    )
+        gather_whole(w_query),
+        gather_whole(w_key),
+        gather_whole(w_value),
+        gather_whole(w_output),
+    )
+    ffn_full = (gather_whole(w_gate), gather_staged(w_up), gather_whole(w_down))
     block_out, saved = layer_forward(
         tokens_in,
         segment_ids,
@@ -340,40 +365,8 @@
         ffn_full[2],
         seq_len,
     )
-    gain_total = lax.psum((gains[0], gains[1], gains[2], gains[3]), ("rep", "fsdp"))
-    lefts = (
-        lax.all_to_all(pairs[0][0], "fsdp", split_axis=1, concat_axis=0, tiled=True),
-        lax.all_to_all(pairs[3][0], "fsdp", split_axis=1, concat_axis=0, tiled=True),
-        lax.all_to_all(pairs[4][0], "fsdp", split_axis=1, concat_axis=0, tiled=True),
-        lax.all_to_all(pairs[6][0], "fsdp", split_axis=1, concat_axis=0, tiled=True),
-    )
-    rights = (
-        lax.all_gather(pairs[0][1], "fsdp", axis=0, tiled=True),
-        lax.all_gather(pairs[1][1], "fsdp", axis=0, tiled=True),
-        lax.all_gather(pairs[2][1], "fsdp", axis=0, tiled=True),
-        lax.all_gather(pairs[3][1], "fsdp", axis=0, tiled=True),
-        lax.all_gather(pairs[4][1], "fsdp", axis=0, tiled=True),
-        lax.all_gather(pairs[5][1], "fsdp", axis=0, tiled=True),
-        lax.all_gather(pairs[6][1], "fsdp", axis=0, tiled=True),
-    )
-    owned = (
-        transposed_times(lefts[0], rights[0]),
-        transposed_times(lefts[0], rights[1]),
-        transposed_times(lefts[0], rights[2]),
-        transposed_times(lefts[1], rights[3]),
-        transposed_times(lefts[2], rights[4]),
-        transposed_times(lefts[2], rights[5]),
-        transposed_times(lefts[3], rights[6]),
-    )
-    grads = (
-        lax.psum(owned[0].astype(jnp.bfloat16), "rep").astype(jnp.float32),
-        lax.psum(owned[1].astype(jnp.bfloat16), "rep").astype(jnp.float32),
-        lax.psum(owned[2].astype(jnp.bfloat16), "rep").astype(jnp.float32),
-        lax.psum(owned[3].astype(jnp.bfloat16), "rep").astype(jnp.float32),
-        lax.psum(owned[4].astype(jnp.bfloat16), "rep").astype(jnp.float32),
-        lax.psum(owned[5].astype(jnp.bfloat16), "rep").astype(jnp.float32),
-        lax.psum(owned[6].astype(jnp.bfloat16), "rep").astype(jnp.float32),
-    )
+    gain_total = sum_gains(gains)
+    grads = tuple(sum_grad(first, second) for first, second in pairs)
     return (
         block_out,
         input_grad,

time: 1090 us -> 1560 us (1.43)
  waiting for transfers between devices: 864 us -> 1290 us
  blocking collectives: 39.8 us -> 82.9 us
    reduce_scatter x0 -> x7, waiting for transfers between devices: none -> 807 us  [sum_grad(): lax.psum_scatter(local, ('fsdp', 'rep'), scatter_dimension=0, tiled=True)]
    all_gather x14 -> x12, waiting for transfers between devices: 730 us -> 479 us  [the longest x6 333 us: gather_whole(): return lax.all_gather(own_piece(shard), ('fsdp', 'rep'), axis=0, tiled=True)]
    all_gather x0 -> x4, blocking collectives: none -> 82.9 us  [the longest x1 40.4 us: sum_gains(): total = jnp.sum(lax.all_gather(packed, ('fsdp', 'rep'), axis=0), axis=0)]
    psum x1 -> x0, waiting for transfers between devices: 70.3 us -> none  [body(): lax.psum(owned[0].astype(jnp.bfloat16), 'rep').astype(jnp.float32)]
    all_to_all x4 -> x0, waiting for transfers between devices: 57.6 us -> none  [the longest x1 22.3 us: body(): lax.all_to_all(pairs[6][0], 'fsdp', split_axis=1, concat_axis=0, tiled=True)]
    psum x1 -> x0, blocking collectives: 39.8 us -> none  [body(): lax.psum((gains[0], gains[1], gains[2], gains[3]), ('rep', 'fsdp'))]
  transfers between devices with their start and end apart: 19 -> 19, of which waited for: 14 -> 19; matrix products, arithmetic and copies ran while one was open for 12% -> 7% of each run, Pallas kernels for 0% -> 0%
where the time goes in v1:
time: 1560 us; the launch traced here: 1550 us
  waiting for transfers between devices  1290 us (83%)
  blocking collectives  82.9 us (5%)
  matrix products  81.7 us (5%)
  local copies, waits for them, and re-layouts  47.8 us (3%)
  other arithmetic  37.4 us (2%)
    reduce_scatter x7, waiting for transfers between devices, sum_grad(): lax.psum_scatter(local, ('fsdp', 'rep'), scatter_dimension=0, tiled=True)  807 us
    all_gather x6, waiting for transfers between devices, gather_whole(): return lax.all_gather(own_piece(shard), ('fsdp', 'rep'), axis=0, tiled=True)  333 us
    all_gather x5, waiting for transfers between devices, sum_grad(): return lax.all_gather(piece, 'rep', axis=0, tiled=True).astype(jnp.float32)  104 us
    all_gather x1, waiting for transfers between devices, gather_staged(): full = lax.all_gather(part, 'rep', axis=1)  42.3 us
    all_gather x1, blocking collectives, sum_gains(): total = jnp.sum(lax.all_gather(packed, ('fsdp', 'rep'), axis=0), axis=0)  40.4 us
  transfers between devices with their start and end apart: 19, of which 19 were waited for; matrix products, arithmetic and copies ran while one was open for 7% of the time, Pallas kernels for 0%

profile of v1, /device:TPU:0, one launch (start us, length us, event | category | flops | bytes accessed | tf_op | source)
XLA Modules:
  0.0 1552.6 jit_solution(3323044329091308585)
XLA Ops:
  13.9 22.7 %all-gather = bf16[128,3072]{1,0:T(8,128)(2,1)} all-gather(bf16[32,3072]{1,0:T(8,128)(2,1)S(1)} %constant_dynamic-slice_fusion.1), channel_id=2, replica_groups=mesh['rep'=8,'fsdp'=4] {'fsdp'}, dimensions={0}, use_global_device_ids=true | all-gather | bytes 983040 | tf_op jit(solution)/shard_map/all_gather | solution.py:290
  42.6 28.4 %all-gather.19.cloned.1.call-done = bf16[1024,1024]{1,0:T(8,128)(2,1)} async-done(((bf16[32,1024]{1,0:T(8,128)(2,1)}), bf16[1024,1024]{1,0:T(8,128)(2,1)}) %all-gather.19.cloned.1.call-update) | async-done | bytes 2097168 | tf_op jit(solution)/shard_map/all_gather | solution.py:286
  74.4 55.1 %all-gather.17.cloned.1.call-done = bf16[1024,1024]{1,0:T(8,128)(2,1)} async-done(((bf16[32,1024]{1,0:T(8,128)(2,1)}), bf16[1024,1024]{1,0:T(8,128)(2,1)}) %all-gather.17.cloned.1.call-update) | async-done | bytes 2097168 | tf_op jit(solution)/shard_map/all_gather | solution.py:286
  132.0 61.5 %all-gather.21.cloned.1.call-done = bf16[1024,2048]{1,0:T(8,128)(2,1)} async-done(((bf16[32,2048]{1,0:T(8,128)(2,1)}), bf16[1024,2048]{1,0:T(8,128)(2,1)}) %all-gather.21.cloned.1.call-update) | async-done | bytes 4194320 | tf_op jit(solution)/shard_map/all_gather | solution.py:286
  203.4 54.0 %all-gather.23.cloned.1.call-done = bf16[2048,1024]{1,0:T(8,128)(2,1)} async-done(((bf16[64,1024]{1,0:T(8,128)(2,1)}), bf16[2048,1024]{1,0:T(8,128)(2,1)}) %all-gather.23.cloned.1.call-update) | async-done | bytes 4194320 | tf_op jit(solution)/shard_map/all_gather | solution.py:286
  261.1 42.3 %all-gather.39.cloned.1.call-done = bf16[4,256,3072]{2,1,0:T(8,128)(2,1)} async-done(((bf16[4,32,3072]{2,1,0:T(8,128)(2,1)}), bf16[4,256,3072]{2,1,0:T(8,128)(2,1)}) %all-gather.39.cloned.1.call-update) | async-done | bytes 6291472 | tf_op jit(solution)/shard_map/all_gather | solution.py:291
  303.4 4.9 fusion.55
  308.3 67.6 %all-gather.25.cloned.1.call-done = bf16[1024,3072]{1,0:T(8,128)(2,1)} async-done(((bf16[32,3072]{1,0:T(8,128)(2,1)}), bf16[1024,3072]{1,0:T(8,128)(2,1)}) %all-gather.25.cloned.1.call-update) | async-done | bytes 6291472 | tf_op jit(solution)/shard_map/all_gather | solution.py:286
  375.8 4.9 fusion.54
  380.8 66.2 %all-gather.27.cloned.1.call-done = bf16[3072,1024]{1,0:T(8,128)(2,1)} async-done(((bf16[96,1024]{1,0:T(8,128)(2,1)}), bf16[3072,1024]{1,0:T(8,128)(2,1)}) %all-gather.27.cloned.1.call-update) | async-done | bytes 6291472 | tf_op jit(solution)/shard_map/all_gather | solution.py:286
  447.0 7.2 multiply_convert_fusion
  456.5 6.1 multiply_reduce_fusion.4
  503.3 5.7 convolution_convert_fusion.2
  509.2 5.5 convolution_convert_fusion.1
  515.7 5.6 convolution_convert_fusion
  542.4 97.8 %reduce-scatter.8.cloned.1.call-done = bf16[32,2048]{1,0:T(8,128)(2,1)} async-done(((bf16[1024,2048]{1,0:T(8,128)(2,1)}), bf16[32,2048]{1,0:T(8,128)(2,1)}) %reduce-scatter.8.cloned.1.call-update) | async-done | bytes 131088 | tf_op jit(solution)/shard_map/reduce_scatter | solution.py:297
  640.3 140.9 %reduce-scatter.14.cloned.1.call-done = bf16[64,1024]{1,0:T(8,128)(2,1)} async-done(((bf16[2048,1024]{1,0:T(8,128)(2,1)}), bf16[64,1024]{1,0:T(8,128)(2,1)}) %reduce-scatter.14.cloned.1.call-update) | async-done | bytes 131088 | tf_op jit(solution)/shard_map/reduce_scatter | solution.py:297
  781.3 116.3 %reduce-scatter.16.cloned.1.call-done = bf16[32,3072]{1,0:T(8,128)(2,1)} async-done(((bf16[1024,3072]{1,0:T(8,128)(2,1)}), bf16[32,3072]{1,0:T(8,128)(2,1)}) %reduce-scatter.16.cloned.1.call-update) | async-done | bytes 196624 | tf_op jit(solution)/shard_map/reduce_scatter | solution.py:297
  897.6 119.5 %reduce-scatter.18.cloned.1.call-done = bf16[32,3072]{1,0:T(8,128)(2,1)} async-done(((bf16[1024,3072]{1,0:T(8,128)(2,1)}), bf16[32,3072]{1,0:T(8,128)(2,1)}) %reduce-scatter.18.cloned.1.call-update) | async-done | bytes 196624 | tf_op jit(solution)/shard_map/reduce_scatter | solution.py:297
  1017.2 119.3 %reduce-scatter.20.cloned.1.call-done = bf16[96,1024]{1,0:T(8,128)(2,1)} async-done(((bf16[3072,1024]{1,0:T(8,128)(2,1)}), bf16[96,1024]{1,0:T(8,128)(2,1)}) %reduce-scatter.20.cloned.1.call-update) | async-done | bytes 196624 | tf_op jit(solution)/shard_map/reduce_scatter | solution.py:297
  1143.4 40.4 %all-gather.3 = f32[32,1,2304]{2,1,0:T(1,128)S(1)} all-gather(f32[1,1,2304]{2,1,0:T(1,128)S(1)} %reshape.315), channel_id=4, replica_groups=mesh['rep'=8,'fsdp'=4] {'fsdp','rep'}, dimensions={0}, use_global_device_ids=true | all-gather | bytes 304128 | tf_op jit(solution)/shard_map/all_gather | solution.py:304
  1186.1 4.5 fusion.3
  1190.6 86.0 %reduce-scatter.10.cloned.1.call-done = bf16[32,1024]{1,0:T(8,128)(2,1)} async-done(((bf16[1024,1024]{1,0:T(8,128)(2,1)}), bf16[32,1024]{1,0:T(8,128)(2,1)}) %reduce-scatter.10.cloned.1.call-update) | async-done | bytes 65552 | tf_op jit(solution)/shard_map/reduce_scatter | solution.py:297
  1276.6 9.4 all_gather.70
  1287.1 126.7 %reduce-scatter.12.cloned.1.call-done = bf16[32,1024]{1,0:T(8,128)(2,1)} async-done(((bf16[1024,1024]{1,0:T(8,128)(2,1)}), bf16[32,1024]{1,0:T(8,128)(2,1)}) %reduce-scatter.12.cloned.1.call-update) | async-done | bytes 65552 | tf_op jit(solution)/shard_map/reduce_scatter | solution.py:297
  1413.8 10.4 all_gather.71
  1425.3 9.5 all-gather.29.cloned.1.call-done
  1437.6 22.4 %all-gather.31.cloned.1.call-done = bf16[512,1024]{1,0:T(8,128)(2,1)} async-done(((bf16[64,1024]{1,0:T(8,128)(2,1)}), bf16[512,1024]{1,0:T(8,128)(2,1)}) %all-gather.31.cloned.1.call-update) | async-done | bytes 1048592 | tf_op jit(solution)/shard_map/all_gather | solution.py:298
  1462.7 24.5 %all-gather.33.cloned.1.call-done = bf16[256,3072]{1,0:T(8,128)(2,1)} async-done(((bf16[32,3072]{1,0:T(8,128)(2,1)}), bf16[256,3072]{1,0:T(8,128)(2,1)}) %all-gather.33.cloned.1.call-update) | async-done | bytes 1572880 | tf_op jit(solution)/shard_map/all_gather | solution.py:298
  1490.7 23.9 %all-gather.35.cloned.1.call-done = bf16[256,3072]{1,0:T(8,128)(2,1)} async-done(((bf16[32,3072]{1,0:T(8,128)(2,1)}), bf16[256,3072]{1,0:T(8,128)(2,1)}) %all-gather.35.cloned.1.call-update) | async-done | bytes 1572880 | tf_op jit(solution)/shard_map/all_gather | solution.py:298
  1514.6 3.6 convert_element_type.169
  1518.2 23.9 %all-gather.37.cloned.1.call-done = bf16[768,1024]{1,0:T(8,128)(2,1)} async-done(((bf16[96,1024]{1,0:T(8,128)(2,1)}), bf16[768,1024]{1,0:T(8,128)(2,1)}) %all-gather.37.cloned.1.call-update) | async-done | bytes 1572880 | tf_op jit(solution)/shard_map/all_gather | solution.py:298
  (270 shorter events, 120.2 us)
Async XLA Ops:
  7.2 63.8 %copy-start.36 = (f32[1024]{0:T(1024)S(1)}, f32[1024]{0:T(1024)}, u32[]{:S(2)}) copy-start(f32[1024]{0:T(1024)} %param.16) | copy-start | bytes 12292
  7.3 63.7 %all-gather.19.cloned.1.call-start = ((), (), s32[]{:S(2)}) async-start(), calls=%async_computation.8 | async-start | bytes 2162688 | tf_op jit(solution)/shard_map/all_gather | solution.py:286
  8.9 120.6 %all-gather.17.cloned.1.call-start = ((), (), s32[]{:S(2)}) async-start(), calls=%async_computation.7 | async-start | bytes 2162688 | tf_op jit(solution)/shard_map/all_gather | solution.py:286
  10.5 183.1 %all-gather.21.cloned.1.call-start = ((), (), s32[]{:S(2)}) async-start(), calls=%async_computation.9 | async-start | bytes 4325376 | tf_op jit(solution)/shard_map/all_gather | solution.py:286
  12.1 245.3 %all-gather.23.cloned.1.call-start = ((), (), s32[]{:S(2)}) async-start(), calls=%async_computation.10 | async-start | bytes 4325376 | tf_op jit(solution)/shard_map/all_gather | solution.py:286
  13.8 289.6 %all-gather.39.cloned.1.call-start = ((), (), s32[]{:S(2)}) async-start(), calls=%async_computation.25 | async-start | bytes 7077888 | tf_op jit(solution)/shard_map/all_gather | solution.py:291
  36.6 339.3 %all-gather.25.cloned.1.call-start = ((), (), s32[]{:S(2)}) async-start(), calls=%async_computation.11 | async-start | bytes 6488064 | tf_op jit(solution)/shard_map/all_gather | solution.py:286
  38.3 408.7 %all-gather.27.cloned.1.call-start = ((), (), s32[]{:S(2)}) async-start(), calls=%async_computation.12 | async-start | bytes 6488064 | tf_op jit(solution)/shard_map/all_gather | solution.py:286
  40.0 600.3 %reduce-scatter.8.cloned.1.call-start = ((), (), s32[]{:S(2)}) async-start(), calls=%async_computation.13 | async-start | bytes 4325376 | tf_op jit(solution)/shard_map/reduce_scatter | solution.py:297
  41.9 151.7 %copy-start.47 = (f32[128]{0:T(128)}, f32[128]{0:T(128)S(1)}, u32[]{:S(2)}) copy-start(f32[128]{0:T(128)S(1)} %add_rsqrt_fusion.3) | copy-start | bytes 1540
  73.1 58.6 %copy-start.59 = (f32[128]{0:T(128)S(1)}, f32[128]{0:T(128)}, u32[]{:S(2)}) copy-start(f32[128]{0:T(128)} %param.18) | copy-start | bytes 1540
  74.1 57.9 %copy-start.10 = (f32[128,8,128]{0,2,1:T(8,128)}, f32[128,8,128]{0,2,1:T(8,128)S(1)}, u32[]{:S(2)}) copy-start(f32[128,8,128]{0,2,1:T(8,128)S(1)} %copy.146) | copy-start | bytes 1572868
  131.6 71.4 %copy-start.26 = (bf16[16,8,8,128]{3,2,1,0:T(8,128)(2,1)}, bf16[16,8,8,128]{3,2,1,0:T(8,128)(2,1)S(1)}, u32[]{:S(2)}) copy-start(bf16[16,8,8,128]{3,2,1,0:T(8,128)(2,1)S(1)} %copy.201) | copy-start | bytes 786436
  131.7 61.9 %copy-start.45 = (f32[128,8]{0,1:T(8,128)}, f32[128,8]{0,1:T(8,128)S(1)}, u32[]{:S(2)}) copy-start(f32[128,8]{0,1:T(8,128)S(1)} %add_rsqrt_fusion.1) | copy-start | bytes 12292
  132.0 70.2 %copy-start.28 = (bf16[128,8,128,1]{0,2,3,1:T(8,128)(2,1)}, bf16[128,8,128,1]{0,2,3,1:T(8,128)(2,1)S(1)}, u32[]{:S(2)}) copy-start(bf16[128,8,128,1]{0,2,3,1:T(8,128)(2,1)S(1)} %fusion.33) | copy-start | bytes 786436
  203.4 57.1 %copy-start.12 = (bf16[8,128,2,128]{3,1,2,0:T(8,128)(2,1)}, bf16[8,128,2,128]{3,1,2,0:T(8,128)(2,1)S(1)}, u32[]{:S(2)}) copy-start(bf16[8,128,2,128]{3,1,2,0:T(8,128)(2,1)S(1)} %convolution_convert_fusion.8) | copy-start | bytes 1572868
  308.3 138.7 %copy-start.34 = (bf16[128,1024]{1,0:T(8,128)(2,1)S(1)}, bf16[128,1024]{1,0:T(8,128)(2,1)}, u32[]{:S(2)}) copy-start(bf16[128,1024]{1,0:T(8,128)(2,1)} %param.29) | copy-start | bytes 786436
  498.7 282.4 %reduce-scatter.14.cloned.1.call-start = ((), (), s32[]{:S(2)}) async-start(), calls=%async_computation.17 | async-start | bytes 4325376 | tf_op jit(solution)/shard_map/reduce_scatter | solution.py:297
  503.2 394.3 %reduce-scatter.16.cloned.1.call-start = ((), (), s32[]{:S(2)}) async-start(), calls=%async_computation.19 | async-start | bytes 6488064 | tf_op jit(solution)/shard_map/reduce_scatter | solution.py:297
  509.0 508.2 %reduce-scatter.18.cloned.1.call-start = ((), (), s32[]{:S(2)}) async-start(), calls=%async_computation.21 | async-start | bytes 6488064 | tf_op jit(solution)/shard_map/reduce_scatter | solution.py:297
  514.8 621.7 %reduce-scatter.20.cloned.1.call-start = ((), (), s32[]{:S(2)}) async-start(), calls=%async_computation.23 | async-start | bytes 6488064 | tf_op jit(solution)/shard_map/reduce_scatter | solution.py:297
  521.4 755.2 %reduce-scatter.10.cloned.1.call-start = ((), (), s32[]{:S(2)}) async-start(), calls=%async_computation.15 | async-start | bytes 2162688 | tf_op jit(solution)/shard_map/reduce_scatter | solution.py:297
  539.7 874.1 %reduce-scatter.12.cloned.1.call-start = ((), (), s32[]{:S(2)}) async-start(), calls=%async_computation.16 | async-start | bytes 2162688 | tf_op jit(solution)/shard_map/reduce_scatter | solution.py:297
  540.1 357.4 %copy-start.30 = (bf16[8,128,128]{2,1,0:T(8,128)(2,1)}, bf16[8,128,128]{2,1,0:T(8,128)(2,1)S(1)}, u32[]{:S(2)}) copy-start(bf16[8,128,128]{2,1,0:T(8,128)(2,1)S(1)} %fusion.4) | copy-start | bytes 786436
  540.2 596.4 %copy-start.33 = (bf16[128,1024]{1,0:T(8,128)(2,1)S(1)}, bf16[128,1024]{1,0:T(8,128)(2,1)}, u32[]{:S(2)}) copy-start(bf16[128,1024]{1,0:T(8,128)(2,1)} %copy-done.32) | copy-start | bytes 786436
  542.3 892.5 %all-gather.29.cloned.1.call-start = ((), (), s32[]{:S(2)}) async-start(), calls=%async_computation.14 | async-start | bytes 1179648 | tf_op jit(solution)/shard_map/all_gather | solution.py:298
  640.2 819.7 %all-gather.31.cloned.1.call-start = ((), (), s32[]{:S(2)}) async-start(), calls=%async_computation.18 | async-start | bytes 1179648 | tf_op jit(solution)/shard_map/all_gather | solution.py:298
  781.2 706.1 %all-gather.33.cloned.1.call-start = ((), (), s32[]{:S(2)}) async-start(), calls=%async_computation.20 | async-start | bytes 1769472 | tf_op jit(solution)/shard_map/all_gather | solution.py:298
  897.6 241.6 %copy-start.31 = (bf16[8,128,128]{2,1,0:T(8,128)(2,1)S(1)}, bf16[8,128,128]{2,1,0:T(8,128)(2,1)}, u32[]{:S(2)}) copy-start(bf16[8,128,128]{2,1,0:T(8,128)(2,1)} %copy-done.30) | copy-start | bytes 786436
  897.6 244.0 %copy-start.23 = (bf16[128,2048]{1,0:T(8,128)(2,1)S(1)}, bf16[128,2048]{1,0:T(8,128)(2,1)}, u32[]{:S(2)}) copy-start(bf16[128,2048]{1,0:T(8,128)(2,1)} %copy-done.22) | copy-start | bytes 1572868
  897.6 617.0 %all-gather.35.cloned.1.call-start = ((), (), s32[]{:S(2)}) async-start(), calls=%async_computation.22 | async-start | bytes 1769472 | tf_op jit(solution)/shard_map/all_gather | solution.py:298
  1017.2 524.9 %all-gather.37.cloned.1.call-start = ((), (), s32[]{:S(2)}) async-start(), calls=%async_computation.24 | async-start | bytes 1769472 | tf_op jit(solution)/shard_map/all_gather | solution.py:298
  (53 other events, 427.9 us)
Sparse Core Ops, SparseCore 0:
  11.5 59.4 all-gather.18
  74.4 55.0 all-gather.16
  132.9 60.5 all-gather.20
  196.8 60.4 all-gather.22
  259.1 44.1 all-gather.38
  306.6 69.1 all-gather.24
  379.3 67.6 all-gather.26
  498.9 141.3 reduce-scatter.7
  642.5 138.6 reduce-scatter.13
  786.7 110.8 reduce-scatter.15
  903.2 113.9 reduce-scatter.17
  1022.6 113.8 reduce-scatter.19
  1139.4 137.1 reduce-scatter.9
  1279.3 134.4 reduce-scatter.11
  1415.5 19.2 all-gather.28
  1436.6 23.3 all-gather.30
  1461.7 25.5 all-gather.32
  1489.0 25.5 all-gather.34
  1516.5 25.5 all-gather.36

commit v2 on v0

--- a/solution.py
+++ b/solution.py
@@ -4,6 +4,8 @@
 import jax
 import jax.numpy as jnp
 from jax import lax
+from jax.experimental import pallas as pl
+from jax.experimental.pallas import tpu as pltpu
 from jax.sharding import PartitionSpec as P
 
 EPS = 1e-06
@@ -277,6 +279,141 @@
     return (input_grad, gains, pairs)
 
 
+SWAPPED = (0, 1, 1, 0, 1, 0, 1)
+
+
+def gather_kernel(count, groups, copies, rounds, *refs):
+    shards = refs[:count]
+    outs = refs[count : 2 * count]
+    pieces = refs[2 * count : 3 * count]
+    local_in, local_out, send_sem, recv_sem = refs[3 * count :]
+    mine = lax.axis_index("rep")
+    group = lax.axis_index("fsdp")
+
+    def flip(index, bit):
+        step = 1 << bit
+        return index + step * (1 - 2 * (lax.rem(index // step, 2)))
+
+    def place(rep, fsdp):
+        return {"rep": rep, "fsdp": fsdp}
+
+    barrier = pltpu.get_barrier_semaphore()
+    for away in range(1, groups):
+        pl.semaphore_signal(
+            barrier,
+            inc=1,
+            device_id=place(mine, lax.rem(group + away, groups)),
+            device_id_type=pl.DeviceIdType.MESH,
+        )
+    for bit in range(rounds):
+        pl.semaphore_signal(
+            barrier,
+            inc=1,
+            device_id=place(flip(mine, bit), group),
+            device_id_type=pl.DeviceIdType.MESH,
+        )
+    pl.semaphore_wait(barrier, groups - 1 + rounds)
+
+    def send(source, target, which, slot, rep, fsdp):
+        copy = pltpu.make_async_remote_copy(
+            src_ref=source,
+            dst_ref=target,
+            send_sem=send_sem.at[which, slot],
+            recv_sem=recv_sem.at[which, slot],
+            device_id=place(rep, fsdp),
+            device_id_type=pl.DeviceIdType.MESH,
+        )
+        copy.start()
+        return copy
+
+    started = []
+    latest = []
+    for which in range(count):
+        stage = []
+        for away in range(1, groups):
+            stage.append(
+                send(
+                    shards[which].at[mine],
+                    outs[which].at[group, mine],
+                    which,
+                    away - 1,
+                    mine,
+                    lax.rem(group + away, groups),
+                )
+            )
+        latest.append(stage)
+        started.extend(stage)
+    loads = []
+    for which in range(count):
+        load = pltpu.make_async_copy(shards[which].at[mine], pieces[which], local_in.at[which])
+        load.start()
+        loads.append(load)
+    stores = []
+    for which in range(count):
+        loads[which].wait()
+        store = pltpu.make_async_copy(
+            pieces[which], outs[which].at[group, mine], local_out.at[which]
+        )
+        store.start()
+        stores.append(store)
+    held = [[mine] for _ in range(count)]
+    slots = [groups - 1] * count
+    orders = []
+    for which in range(count):
+        upper = list(range(1, rounds))
+        if SWAPPED[which % len(SWAPPED)]:
+            upper = upper[::-1]
+        orders.append(upper + [0])
+    for tick in range(count + rounds):
+        for which in range(count):
+            turn = tick - which
+            if turn < 0 or turn > rounds:
+                continue
+            for copy in latest[which]:
+                copy.wait_recv()
+            if turn == 0:
+                stores[which].wait()
+            if turn == rounds:
+                continue
+            bit = orders[which][turn]
+            stage = []
+            for rep in held[which]:
+                part = outs[which].at[:, rep]
+                stage.append(send(part, part, which, slots[which], flip(mine, bit), group))
+                slots[which] += 1
+            held[which] = held[which] + [flip(rep, bit) for rep in held[which]]
+            latest[which] = stage
+            started.extend(stage)
+    for copy in started:
+        copy.wait_send()
+
+
+def gather_weights(shards):
+    count = len(shards)
+    groups = lax.axis_size("fsdp")
+    copies = lax.axis_size("rep")
+    rounds = copies.bit_length() - 1
+    slots = groups - 1 + copies - 1
+    split = [shard.reshape(copies, -1, shard.shape[1]) for shard in shards]
+    anywhere = pl.BlockSpec(memory_space=pl.ANY)
+    full = pl.pallas_call(
+        partial(gather_kernel, count, groups, copies, rounds),
+        out_shape=[jax.ShapeDtypeStruct((groups, *part.shape), part.dtype) for part in split],
+        in_specs=[anywhere] * count,
+        out_specs=[anywhere] * count,
+        scratch_shapes=[pltpu.VMEM(part.shape[1:], part.dtype) for part in split]
+        + [
+            pltpu.SemaphoreType.DMA((count,)),
+            pltpu.SemaphoreType.DMA((count,)),
+            pltpu.SemaphoreType.DMA((count, slots)),
+            pltpu.SemaphoreType.DMA((count, slots)),
+        ],
+        compiler_params=pltpu.CompilerParams(collective_id=0, has_side_effects=True),
+        name="gather_weights",
+    )(*split)
+    return [whole.reshape(-1, whole.shape[-1]) for whole in full]
+
+
 def body(
     tokens_in,
     input_gain,
@@ -295,17 +432,9 @@
     out_cotangent,
 ):
     seq_len = tokens_in.shape[0]
-    attn_full = (
-        lax.all_gather(w_query, "fsdp", axis=0, tiled=True),
-        lax.all_gather(w_key, "fsdp", axis=0, tiled=True),
-        lax.all_gather(w_value, "fsdp", axis=0, tiled=True),
-        lax.all_gather(w_output, "fsdp", axis=0, tiled=True),
-    )
-    ffn_full = (
-        lax.all_gather(w_gate, "fsdp", axis=0, tiled=True),
-        lax.all_gather(w_up, "fsdp", axis=0, tiled=True),
-        lax.all_gather(w_down, "fsdp", axis=0, tiled=True),
-    )
+    gathered = gather_weights((w_query, w_key, w_value, w_output, w_gate, w_up, w_down))
+    attn_full = tuple(gathered[:4])
+    ffn_full = tuple(gathered[4:])
     block_out, saved = layer_forward(
         tokens_in,
         segment_ids,

time: 1090 us -> 800 us (0.73)
  waiting for transfers between devices: 864 us -> 355 us
  Pallas kernels: 0 us -> 245 us
  matrix products: 84.4 us -> 70.2 us
  starting transfers between devices: 15.2 us -> 27.8 us
  local copies, waits for them, and re-layouts: 35.9 us -> 23.5 us
    all_gather x7 -> x0, waiting for transfers between devices: 567 us -> none  [the longest x1 111 us: body(): lax.all_gather(w_gate, 'fsdp', axis=0, tiled=True)]
    pallas_call x0 -> x1, Pallas kernels: none -> 245 us  [gather_weights(): pl.pallas_call(partial(gather_kernel, count, groups, copies, rounds), out...]
    all_gather x1, waiting for transfers between devices: 0.01 us -> 31.6 us  [body(): lax.all_gather(pairs[2][1], 'fsdp', axis=0, tiled=True)]
    all_gather x1, waiting for transfers between devices: 0.01 us -> 30.7 us  [body(): lax.all_gather(pairs[6][1], 'fsdp', axis=0, tiled=True)]
    all_gather x1, waiting for transfers between devices: 0.02 us -> 24.7 us  [body(): lax.all_gather(pairs[3][1], 'fsdp', axis=0, tiled=True)]
    all_to_all x1, waiting for transfers between devices: 22.3 us -> 0.01 us  [body(): lax.all_to_all(pairs[6][0], 'fsdp', split_axis=1, concat_axis=0, tiled=True)]
  transfers between devices with their start and end apart: 19 -> 12, of which waited for: 14 -> 9; matrix products, arithmetic and copies ran while one was open for 12% -> 5% of each run, Pallas kernels for 0% -> 0%
where the time goes in v2:
time: 800 us; the launch traced here: 799 us
  waiting for transfers between devices  355 us (44%)
  Pallas kernels  245 us (31%)
  matrix products  70.2 us (9%)
  blocking collectives  40 us (5%)
  starting transfers between devices  27.8 us (3%)
  local copies, waits for them, and re-layouts  23.5 us (3%)
  other arithmetic  22.7 us (3%)
  between operations  15 us (2%)
    pallas_call x1, Pallas kernels, gather_weights(): pl.pallas_call(partial(gather_kernel, count, groups, copies, rounds), out...  245 us
    psum x1, waiting for transfers between devices, body(): lax.psum(owned[0].astype(jnp.bfloat16), 'rep').astype(jnp.float32)  69.5 us
    all_gather x1, waiting for transfers between devices, body(): lax.all_gather(pairs[4][1], 'fsdp', axis=0, tiled=True)  60.3 us
    all_gather x1, waiting for transfers between devices, body(): lax.all_gather(pairs[5][1], 'fsdp', axis=0, tiled=True)  60.2 us
    all_gather x1, waiting for transfers between devices, body(): lax.all_gather(pairs[0][1], 'fsdp', axis=0, tiled=True)  44.1 us
    psum x1, blocking collectives, body(): lax.psum((gains[0], gains[1], gains[2], gains[3]), ('rep', 'fsdp'))  40 us
    all_gather x1, waiting for transfers between devices, body(): lax.all_gather(pairs[2][1], 'fsdp', axis=0, tiled=True)  31.6 us
    all_gather x1, waiting for transfers between devices, body(): lax.all_gather(pairs[6][1], 'fsdp', axis=0, tiled=True)  30.7 us
  transfers between devices with their start and end apart: 12, of which 9 were waited for; matrix products, arithmetic and copies ran while one was open for 5% of the time, Pallas kernels for 0%

profile of v2, /device:TPU:0, one launch (start us, length us, event | category | flops | bytes accessed | tf_op | source)
XLA Modules:
  0.0 799.0 jit_solution(17072519125710909477)
XLA Ops:
  9.4 245.2 %gather_weights.1 = (bf16[4,8,32,2048]{3,2,1,0:T(8,128)(2,1)}, bf16[4,8,32,1024]{3,2,1,0:T(8,128)(2,1)}, bf16[4,8,32,1024]{3,2,1,0:T(8,128)(2,1)}, bf16[4,8,64,1...) custom-call(bf16[8,32,2048]{2,1,0:T(8,128)(2,1)} %bitcast.221, ...), custom_call_target="tpu_custom_call" | custom-call | tf_op jit(solution)/shard_map/gather_weights/pallas_call | solution.py:399
  257.0 2.6 copy.41
  263.3 6.4 copy.42
  269.7 3.5 multiply_reduce_fusion.3
  283.5 4.1 multiply_convert_fusion
  287.6 6.0 fusion.41
  293.6 6.1 multiply_reduce_fusion.4
  301.4 4.8 convolution_convert_fusion.3
  321.8 13.6 %all-to-all-start = ((bf16[128,4,256]{2,0,1:T(8,128)(2,1)}), bf16[128,4,256]{2,0,1:T(8,128)(2,1)S(1)}, u32[]{:S(2)}, u32[]{:S(2)}) async-start(bf16[128,4,256]{2,0,1:T(8,128)(2,1)} %bitcast.170), calls=%async_computation | async-start | bytes 524288 | tf_op jit(solution)/shard_map/all_to_all | solution.py:474
  336.4 14.8 %all-to-all-done = bf16[128,4,256]{2,0,1:T(8,128)(2,1)S(1)} async-done(((bf16[128,4,256]{2,0,1:T(8,128)(2,1)}), bf16[128,4,256]{2,0,1:T(8,128)(2,1)S(1)}, u32[]{:S(2)}, u32[]{:S(2)}) %all-to-all-start) | async-done | bytes 262176 | tf_op jit(solution)/shard_map/all_to_all | solution.py:474
  351.3 6.2 all-to-all-start.1
  358.5 16.0 %all-to-all-done.1 = bf16[128,4,512]{2,0,1:T(8,128)(2,1)S(1)} async-done(((bf16[128,4,512]{2,0,1:T(8,128)(2,1)}), bf16[128,4,512]{2,0,1:T(8,128)(2,1)S(1)}, u32[]{:S(2)}, u32[]{:S(2)}) %all-to-all-start.1) | async-done | bytes 524320 | tf_op jit(solution)/shard_map/all_to_all | solution.py:475
  374.4 4.2 all-to-all-start.3
  379.4 2.5 convolution_convert_fusion.7
  381.9 24.7 %all-gather.14.cloned.1.call-done = bf16[512,1024]{1,0:T(8,128)(2,1)} async-done(((bf16[128,1024]{1,0:T(8,128)(2,1)}), bf16[512,1024]{1,0:T(8,128)(2,1)}) %all-gather.14.cloned.1.call-update) | async-done | bytes 1048592 | tf_op jit(solution)/shard_map/all_gather | solution.py:483
  406.6 2.9 convolution_convert_fusion.5
  409.5 3.4 all-to-all-start.2
  413.0 30.7 %all-gather.20.cloned.1.call-done = bf16[512,1024]{1,0:T(8,128)(2,1)} async-done(((bf16[128,1024]{1,0:T(8,128)(2,1)}), bf16[512,1024]{1,0:T(8,128)(2,1)}) %all-gather.20.cloned.1.call-update) | async-done | bytes 1048592 | tf_op jit(solution)/shard_map/all_gather | solution.py:486
  443.7 3.4 convolution_convert_fusion.4
  447.0 31.6 %all-gather.12.cloned.1.call-done = bf16[512,1024]{0,1:T(8,128)(2,1)} async-done(((bf16[128,1024]{0,1:T(8,128)(2,1)}), bf16[512,1024]{0,1:T(8,128)(2,1)}) %all-gather.12.cloned.1.call-update) | async-done | bytes 1048592 | tf_op jit(solution)/shard_map/all_gather | solution.py:482
  478.6 2.5 convolution_convert_fusion.6
  481.1 44.1 %all-gather.8.cloned.1.call-done = bf16[512,2048]{0,1:T(8,128)(2,1)} async-done(((bf16[128,2048]{0,1:T(8,128)(2,1)}), bf16[512,2048]{0,1:T(8,128)(2,1)}) %all-gather.8.cloned.1.call-update) | async-done | bytes 2097168 | tf_op jit(solution)/shard_map/all_gather | solution.py:480
  525.2 3.3 convolution_convert_fusion.2
  528.5 60.3 %all-gather.16.cloned.1.call-done = bf16[512,3072]{1,0:T(8,128)(2,1)} async-done(((bf16[128,3072]{1,0:T(8,128)(2,1)}), bf16[512,3072]{1,0:T(8,128)(2,1)}) %all-gather.16.cloned.1.call-update) | async-done | bytes 3145744 | tf_op jit(solution)/shard_map/all_gather | solution.py:484
  588.9 4.0 convolution_convert_fusion.1
  592.9 60.2 %all-gather.18.cloned.1.call-done = bf16[512,3072]{1,0:T(8,128)(2,1)} async-done(((bf16[128,3072]{1,0:T(8,128)(2,1)}), bf16[512,3072]{1,0:T(8,128)(2,1)}) %all-gather.18.cloned.1.call-update) | async-done | bytes 3145744 | tf_op jit(solution)/shard_map/all_gather | solution.py:485
  653.1 4.0 convolution_convert_fusion
  659.6 2.8 fusion.43
  664.3 40.0 %all-reduce = (f32[1024]{0:T(1024)}, f32[128]{0:T(128)}, f32[128]{0:T(128)}, f32[1024]{0:T(1024)}) all-reduce(f32[1024]{0:T(1024)S(1)} %get-tuple-element.33, f32[128]{0:T(128)S(1)} %get-tuple-element.27, f32[128]{0:T(128)S(1)} %copy-done.58, f32[1024]{0:T(1024)S(1)} %copy-done.44), channel_id=1, replica_groups=mesh['rep'=8,'fsdp'=4] {'rep','fsdp'}, use_global_device_ids=true, to_apply=%region_12.13 | all-reduce | flops 2304 | bytes 18432 | tf_op jit(solution)/shard_map/psum | solution.py:472
  705.4 4.5 fusion.3
  709.9 69.5 %all-reduce.4.cloned.1.call-done = (bf16[256,2048]{1,0:T(8,128)(2,1)}, bf16[256,1024]{1,0:T(8,128)(2,1)}, bf16[256,1024]{1,0:T(8,128)(2,1)}, bf16[512,1024]{1,0:...) async-done(((bf16[256,2048]{1,0:T(8,128)(2,1)}, bf16[256,1024]{1,0:T(8,128)(2,1)}, bf16[256,1024]{1,0:T(8,128)(2,1)}, ...) | async-done | bytes 7864336 | tf_op jit(solution)/shard_map/psum | solution.py:498
  779.4 2.9 convert_element_type.157
  (213 shorter events, 53.0 us)
Async XLA Ops:
  7.2 372.2 %all-gather.10.cloned.1.call-start = ((), (), s32[]{:S(2)}) async-start(), calls=%async_computation.5 | async-start | bytes 1310720 | tf_op jit(solution)/shard_map/all_gather | solution.py:481
  8.3 246.3 %copy-start.53 = (f32[128]{0:T(128)}, f32[128]{0:T(128)S(1)}, u32[]{:S(2)}) copy-start(f32[128]{0:T(128)S(1)} %add_rsqrt_fusion.3) | copy-start | bytes 1540
  9.4 260.3 %copy-start.6 = (bf16[128,1024]{1,0:T(8,128)(2,1)}, bf16[128,1024]{1,0:T(8,128)(2,1)S(1)}, u32[]{:S(2)}) copy-start(bf16[128,1024]{1,0:T(8,128)(2,1)S(1)} %fusion.14) | copy-start | bytes 786436
  256.9 18.4 %copy-start.19 = (bf16[16,8,8,128]{3,2,1,0:T(8,128)(2,1)}, bf16[16,8,8,128]{3,2,1,0:T(8,128)(2,1)S(1)}, u32[]{:S(2)}) copy-start(bf16[16,8,8,128]{3,2,1,0:T(8,128)(2,1)S(1)} %copy.80) | copy-start | bytes 786436
  259.5 3.8 copy-start.59
  274.4 4.3 slice-start.2
  275.3 3.9 slice-start.3
  293.6 6.9 copy-start.24
  293.6 6.9 copy-start.41
  293.6 6.9 copy-start.51
  312.5 3.7 copy-start.9
  312.5 94.1 %all-gather.14.cloned.1.call-start = ((), (), s32[]{:S(2)}) async-start(), calls=%async_computation.7 | async-start | bytes 1310720 | tf_op jit(solution)/shard_map/all_gather | solution.py:483
  313.3 130.4 %all-gather.20.cloned.1.call-start = ((), (), s32[]{:S(2)}) async-start(), calls=%async_computation.10 | async-start | bytes 1310720 | tf_op jit(solution)/shard_map/all_gather | solution.py:486
  314.0 164.6 %all-gather.12.cloned.1.call-start = ((), (), s32[]{:S(2)}) async-start(), calls=%async_computation.6 | async-start | bytes 1310720 | tf_op jit(solution)/shard_map/all_gather | solution.py:482
  316.1 209.1 %all-gather.8.cloned.1.call-start = ((), (), s32[]{:S(2)}) async-start(), calls=%async_computation.4 | async-start | bytes 2621440 | tf_op jit(solution)/shard_map/all_gather | solution.py:480
  319.7 15.7 %copy-start.13 = (bf16[8,128,2,128]{3,1,2,0:T(8,128)(2,1)S(1)}, bf16[8,128,2,128]{3,1,2,0:T(8,128)(2,1)}, u32[]{:S(2)}) copy-start(bf16[8,128,2,128]{3,1,2,0:T(8,128)(2,1)} %copy-done.12) | copy-start | bytes 1572868
  319.7 269.1 %all-gather.16.cloned.1.call-start = ((), (), s32[]{:S(2)}) async-start(), calls=%async_computation.8 | async-start | bytes 3932160 | tf_op jit(solution)/shard_map/all_gather | solution.py:484
  320.3 37.2 %copy-start.17 = (bf16[128,3072]{1,0:T(8,128)(2,1)S(1)}, bf16[128,3072]{1,0:T(8,128)(2,1)}, u32[]{:S(2)}) copy-start(bf16[128,3072]{1,0:T(8,128)(2,1)} %get-tuple-element.50) | copy-start | bytes 2359300
  320.3 332.8 %all-gather.18.cloned.1.call-start = ((), (), s32[]{:S(2)}) async-start(), calls=%async_computation.9 | async-start | bytes 3932160 | tf_op jit(solution)/shard_map/all_gather | solution.py:485
  321.8 29.5 %all-to-all-start = ((bf16[128,4,256]{2,0,1:T(8,128)(2,1)}), bf16[128,4,256]{2,0,1:T(8,128)(2,1)S(1)}, u32[]{:S(2)}, u32[]{:S(2)}) async-start(bf16[128,4,256]{2,0,1:T(8,128)(2,1)} %bitcast.170), calls=%async_computation | async-start | bytes 524288 | tf_op jit(solution)/shard_map/all_to_all | solution.py:474
  351.3 23.2 %all-to-all-start.1 = ((bf16[128,4,512]{2,0,1:T(8,128)(2,1)}), bf16[128,4,512]{2,0,1:T(8,128)(2,1)S(1)}, u32[]{:S(2)}, u32[]{:S(2)}) async-start(bf16[128,4,512]{2,0,1:T(8,128)(2,1)} %copy.55), calls=%async_computation.1 | async-start | bytes 1048576 | tf_op jit(solution)/shard_map/all_to_all | solution.py:475
  374.4 35.1 %all-to-all-start.3 = ((bf16[128,4,768]{2,0,1:T(8,128)(2,1)}), bf16[128,4,768]{2,0,1:T(8,128)(2,1)S(1)}, u32[]{:S(2)}, u32[]{:S(2)}) async-start(bf16[128,4,768]{2,0,1:T(8,128)(2,1)} %bitcast.168), calls=%async_computation.3 | async-start | bytes 1572864 | tf_op jit(solution)/shard_map/all_to_all | solution.py:477
  409.5 119.0 %all-to-all-start.2 = ((bf16[128,4,256]{2,0,1:T(8,128)(2,1)}), bf16[128,4,256]{2,0,1:T(8,128)(2,1)S(1)}, u32[]{:S(2)}, u32[]{:S(2)}) async-start(bf16[128,4,256]{2,0,1:T(8,128)(2,1)} %bitcast.169), calls=%async_computation.2 | async-start | bytes 524288 | tf_op jit(solution)/shard_map/all_to_all | solution.py:476
  412.9 366.5 %all-reduce.4.cloned.1.call-start = ((), (), s32[]{:S(2)}) async-start(), calls=%async_computation.11 | async-start | bytes 15728640 | tf_op jit(solution)/shard_map/psum | solution.py:498
  658.8 3.7 copy-start
  662.6 41.8 %copy-start.16 = (f32[128,1024]{1,0:T(8,128)S(1)}, f32[128,1024]{1,0:T(8,128)}, u32[]{:S(2)}) copy-start(f32[128,1024]{1,0:T(8,128)} %copy-done.15) | copy-start | bytes 1572868
  662.6 41.8 %copy-start.25 = (bf16[128,1024]{1,0:T(8,128)(2,1)S(1)}, bf16[128,1024]{1,0:T(8,128)(2,1)}, u32[]{:S(2)}) copy-start(bf16[128,1024]{1,0:T(8,128)(2,1)} %param.29) | copy-start | bytes 786436
  662.6 41.8 %copy-start.42 = (f32[1024]{0:T(1024)S(1)}, f32[1024]{0:T(1024)}, u32[]{:S(2)}) copy-start(f32[1024]{0:T(1024)} %param.23) | copy-start | bytes 12292
  662.6 41.8 %copy-start.52 = (f32[128]{0:T(128)S(1)}, f32[128]{0:T(128)}, u32[]{:S(2)}) copy-start(f32[128]{0:T(128)} %copy-done.50) | copy-start | bytes 1540
  662.6 41.8 %copy-start.57 = (f32[128]{0:T(128)S(1)}, f32[128]{0:T(128)}, u32[]{:S(2)}) copy-start(f32[128]{0:T(128)} %copy-done.56) | copy-start | bytes 1540
  664.3 41.1 %copy-start.18 = (bf16[128,3072]{1,0:T(8,128)(2,1)S(1)}, bf16[128,3072]{1,0:T(8,128)(2,1)}, u32[]{:S(2)}) copy-start(bf16[128,3072]{1,0:T(8,128)(2,1)} %get-tuple-element.50) | copy-start | bytes 2359300
  779.4 4.0 copy-start.31
  (46 other events, 84.7 us)
Sparse Core Ops, SparseCore 0:
  312.6 56.0 all-gather.9
  370.8 35.7 all-gather.13
  408.2 35.4 all-gather.19
  445.7 32.9 all-gather.11
  480.6 44.5 all-gather.7
  527.2 61.6 all-gather.15
  591.0 62.0 all-gather.17
  658.4 120.9 all-reduce.3

commit v3 on v2

--- a/solution.py
+++ b/solution.py
@@ -409,6 +409,11 @@
             pltpu.SemaphoreType.DMA((count, slots)),
         ],
         compiler_params=pltpu.CompilerParams(collective_id=0, has_side_effects=True),
+        cost_estimate=pl.CostEstimate(
+            flops=0,
+            transcendentals=0,
+            bytes_accessed=8 * groups * sum(2 * shard.size for shard in shards),
+        ),
         name="gather_weights",
     )(*split)
     return [whole.reshape(-1, whole.shape[-1]) for whole in full]
@@ -433,6 +438,8 @@
 ):
     seq_len = tokens_in.shape[0]
     gathered = gather_weights((w_query, w_key, w_value, w_output, w_gate, w_up, w_down))
+    cotangent_full = lax.all_gather(out_cotangent, "fsdp", axis=0, tiled=True)
+    gathered, cotangent_full = lax.optimization_barrier((gathered, cotangent_full))
     attn_full = tuple(gathered[:4])
     ffn_full = tuple(gathered[4:])
     block_out, saved = layer_forward(
@@ -476,14 +483,15 @@
         lax.all_to_all(pairs[4][0], "fsdp", split_axis=1, concat_axis=0, tiled=True),
         lax.all_to_all(pairs[6][0], "fsdp", split_axis=1, concat_axis=0, tiled=True),
     )
-    rights = (
-        lax.all_gather(pairs[0][1], "fsdp", axis=0, tiled=True),
-        lax.all_gather(pairs[1][1], "fsdp", axis=0, tiled=True),
-        lax.all_gather(pairs[2][1], "fsdp", axis=0, tiled=True),
-        lax.all_gather(pairs[3][1], "fsdp", axis=0, tiled=True),
-        lax.all_gather(pairs[4][1], "fsdp", axis=0, tiled=True),
-        lax.all_gather(pairs[5][1], "fsdp", axis=0, tiled=True),
-        lax.all_gather(pairs[6][1], "fsdp", axis=0, tiled=True),
+    early = tuple(
+        lax.all_gather(pairs[at][1], "fsdp", axis=0, tiled=True) for at in (4, 5, 3)
+    )
+    late, early = lax.optimization_barrier((tuple(pairs[at][1] for at in range(3)), early))
+    rights = tuple(lax.all_gather(part, "fsdp", axis=0, tiled=True) for part in late) + (
+        early[2],
+        early[0],
+        early[1],
+        cotangent_full,
     )
     owned = (
         transposed_times(lefts[0], rights[0]),

time: 800 us -> 747 us (0.934)
  waiting for transfers between devices: 355 us -> 283 us
  local copies, waits for them, and re-layouts: 23.5 us -> 46 us
  starting transfers between devices: 27.8 us -> 16.7 us
  other arithmetic: 22.7 us -> 31.8 us
    all_gather x7, waiting for transfers between devices: 252 us -> 155 us  [the longest x3 115 us: body(): lax.all_gather(pairs[at][1], 'fsdp', axis=0, tiled=True)]
    all_to_all x1, waiting for transfers between devices: 0.01 us -> 21.1 us  [body(): lax.all_to_all(pairs[6][0], 'fsdp', split_axis=1, concat_axis=0, tiled=True)]
    all_to_all x1, waiting for transfers between devices: 14.8 us -> 0.95 us  [body(): lax.all_to_all(pairs[0][0], 'fsdp', split_axis=1, concat_axis=0, tiled=True)]
    mul x0 -> x11, local copies, waits for them, and re-layouts: none -> 13.2 us  [the longest x3 5.6 us: layer_forward(): queries * q_scale * q_gain]
    all_to_all x1, waiting for transfers between devices: 0.01 us -> 13.1 us  [body(): lax.all_to_all(pairs[4][0], 'fsdp', split_axis=1, concat_axis=0, tiled=True)]
    all_to_all x1, starting transfers between devices: 13.6 us -> 3.41 us  [body(): lax.all_to_all(pairs[0][0], 'fsdp', split_axis=1, concat_axis=0, tiled=True)]
    dot_general x2 -> x0, local copies, waits for them, and re-layouts: 8.96 us -> none  [the longest x1 6.4 us: layer_forward(): jnp.dot(normed, w_query, preferred_element_type=jnp.float32)]
  transfers between devices with their start and end apart: 12 -> 12, of which waited for: 9 -> 8; matrix products, arithmetic and copies ran while one was open for 5% -> 11% of each run, Pallas kernels for 0% -> 33%
where the time goes in v3:
time: 747 us; the launch traced here: 746 us
  waiting for transfers between devices  283 us (38%)
  Pallas kernels  249 us (33%)
  matrix products  64 us (9%)
  local copies, waits for them, and re-layouts  46 us (6%)
  blocking collectives  39.9 us (5%)
  other arithmetic  31.8 us (4%)
  starting transfers between devices  16.7 us (2%)
  between operations  15.1 us (2%)
    pallas_call x1, Pallas kernels, gather_weights(): pl.pallas_call(partial(gather_kernel, count, groups, copies, rounds), out...  249 us
    all_gather x3, waiting for transfers between devices, body(): lax.all_gather(pairs[at][1], 'fsdp', axis=0, tiled=True)  115 us
    psum x1, waiting for transfers between devices, body(): lax.psum(owned[0].astype(jnp.bfloat16), 'rep').astype(jnp.float32)  70.9 us
    all_gather x3, waiting for transfers between devices, body(): lax.all_gather(part, 'fsdp', axis=0, tiled=True)  40 us
    psum x1, blocking collectives, body(): lax.psum((gains[0], gains[1], gains[2], gains[3]), ('rep', 'fsdp'))  39.9 us
    dot_general x7, matrix products, times_transposed(): lax.dot_general(first, second, (((1,), (1,)), ((), ())), preferred_elemen...  26 us
    all_to_all x1, waiting for transfers between devices, body(): lax.all_to_all(pairs[6][0], 'fsdp', split_axis=1, concat_axis=0, tiled=True)  21.1 us
    all_to_all x1, waiting for transfers between devices, body(): lax.all_to_all(pairs[3][0], 'fsdp', split_axis=1, concat_axis=0, tiled=True)  19.5 us
  transfers between devices with their start and end apart: 12, of which 8 were waited for; matrix products, arithmetic and copies ran while one was open for 11% of the time, Pallas kernels for 33%

profile of v3, /device:TPU:0, one launch (start us, length us, event | category | flops | bytes accessed | tf_op | source)
XLA Modules:
  0.0 745.7 jit_solution(986939616078080000)
XLA Ops:
  8.6 249.3 %gather_weights.1 = (bf16[4,8,32,2048]{3,2,1,0:T(8,128)(2,1)}, bf16[4,8,32,1024]{3,2,1,0:T(8,128)(2,1)}, bf16[4,8,32,1024]{3,2,1,0:T(8,128)(2,1)}, bf16[4,8,64,1...) custom-call(bf16[8,32,2048]{2,1,0:T(8,128)(2,1)} %bitcast.281, ...), custom_call_target="tpu_custom_call" | custom-call | bytes 251658240 | tf_op jit(solution)/shard_map/gather_weights/pallas_call | solution.py:399
  261.8 2.9 fusion.44
  278.4 4.1 multiply_convert_fusion
  282.5 6.1 fusion.47
  288.6 6.2 multiply_reduce_fusion.4
  304.3 4.6 convolution_convert_fusion.3
  314.8 2.6 copy.172
  320.4 2.4 copy.174
  322.8 2.4 copy.175
  325.2 2.5 multiply_reduce_fusion
  328.4 2.5 copy.210
  332.8 2.5 copy.178
  344.7 2.7 pad_maximum_fusion
  353.7 50.6 %all-gather.10.cloned.1.call-done = bf16[512,3072]{1,0:T(8,128)(2,1)} async-done(((bf16[128,3072]{1,0:T(8,128)(2,1)}), bf16[512,3072]{1,0:T(8,128)(2,1)}) %all-gather.10.cloned.1.call-update) | async-done | bytes 3145744 | tf_op jit(solution)/shard_map/all_gather | solution.py:487
  404.3 64.1 %all-gather.12.cloned.1.call-done = bf16[512,3072]{1,0:T(8,128)(2,1)} async-done(((bf16[128,3072]{1,0:T(8,128)(2,1)}), bf16[512,3072]{1,0:T(8,128)(2,1)}) %all-gather.12.cloned.1.call-update) | async-done | bytes 3145744 | tf_op jit(solution)/shard_map/all_gather | solution.py:487
  469.8 3.5 all-to-all-start.2
  474.3 13.1 %all-to-all-done.2 = bf16[128,4,256]{2,0,1:T(8,128)(2,1)S(1)} async-done(((bf16[128,4,256]{2,0,1:T(8,128)(2,1)}), bf16[128,4,256]{2,0,1:T(8,128)(2,1)S(1)}, u32[]{:S(2)}, u32[]{:S(2)}) %all-to-all-start.2) | async-done | bytes 262176 | tf_op jit(solution)/shard_map/all_to_all | solution.py:483
  487.3 5.8 all-to-all-start.3
  494.9 21.1 %all-to-all-done.3 = bf16[128,4,768]{2,0,1:T(8,128)(2,1)S(1)} async-done(((bf16[128,4,768]{2,0,1:T(8,128)(2,1)}), bf16[128,4,768]{2,0,1:T(8,128)(2,1)S(1)}, u32[]{:S(2)}, u32[]{:S(2)}) %all-to-all-start.3) | async-done | bytes 786464 | tf_op jit(solution)/shard_map/all_to_all | solution.py:484
  516.0 3.7 all-to-all-start.1
  524.8 19.5 %all-to-all-done.1 = bf16[128,4,512]{2,0,1:T(8,128)(2,1)S(1)} async-done(((bf16[128,4,512]{2,0,1:T(8,128)(2,1)}), bf16[128,4,512]{2,0,1:T(8,128)(2,1)S(1)}, u32[]{:S(2)}, u32[]{:S(2)}) %all-to-all-start.1) | async-done | bytes 524320 | tf_op jit(solution)/shard_map/all_to_all | solution.py:482
  544.2 3.4 all-to-all-start
  549.4 4.0 convolution_convert_fusion.1
  554.4 2.5 convolution_convert_fusion.6
  556.9 2.5 convolution_convert_fusion.7
  559.4 40.0 %all-gather.16.cloned.1.call-done = bf16[512,2048]{1,0:T(8,128)(2,1)} async-done(((bf16[128,2048]{1,0:T(8,128)(2,1)}), bf16[512,2048]{1,0:T(8,128)(2,1)}) %all-gather.16.cloned.1.call-update) | async-done | bytes 2097168 | tf_op jit(solution)/shard_map/all_gather | solution.py:490
  599.4 3.3 convolution_convert_fusion.2
  603.6 2.6 fusion.49
  609.2 39.9 %all-reduce = (f32[1024]{0:T(1024)}, f32[128]{0:T(128)}, f32[128]{0:T(128)}, f32[1024]{0:T(1024)}) all-reduce(f32[1024]{0:T(1024)S(1)} %get-tuple-element.61, f32[128]{0:T(128)S(1)} %copy-done.77, f32[128]{0:T(128)S(1)} %copy-done.81, f32[1024]{0:T(1024)S(1)} %copy-done.65), channel_id=1, replica_groups=mesh['rep'=8,'fsdp'=4] {'rep','fsdp'}, use_global_device_ids=true, to_apply=%region_12.13 | all-reduce | flops 2304 | bytes 18432 | tf_op jit(solution)/shard_map/psum | solution.py:479
  650.2 4.9 fusion.3
  655.1 70.9 %all-reduce.4.cloned.1.call-done = (bf16[256,2048]{1,0:T(8,128)(2,1)}, bf16[256,1024]{1,0:T(8,128)(2,1)}, bf16[256,1024]{1,0:T(8,128)(2,1)}, bf16[512,1024]{1,0:...) async-done(((bf16[256,2048]{1,0:T(8,128)(2,1)}, bf16[256,1024]{1,0:T(8,128)(2,1)}, bf16[256,1024]{1,0:T(8,128)(2,1)}, ...) | async-done | bytes 7864336 | tf_op jit(solution)/shard_map/psum | solution.py:506
  725.9 3.6 convert_element_type.174
  (287 shorter events, 80.8 us)
Async XLA Ops:
  7.2 251.4 %all-gather.8.cloned.1.call-start = ((), (), s32[]{:S(2)}) async-start(), calls=%async_computation.4 | async-start | bytes 1310720 | tf_op jit(solution)/shard_map/all_gather | solution.py:441
  7.9 345.8 %all-gather.14.cloned.1.call-start = ((), (), s32[]{:S(2)}) async-start(), calls=%async_computation.7 | async-start | bytes 1310720 | tf_op jit(solution)/shard_map/all_gather | solution.py:487
  8.6 249.6 %copy-start.6 = (bf16[128,1024]{1,0:T(8,128)(2,1)S(1)}, bf16[128,1024]{1,0:T(8,128)(2,1)}, u32[]{:S(2)}) copy-start(bf16[128,1024]{1,0:T(8,128)(2,1)} %param.15) | copy-start | bytes 786436
  8.6 249.7 %copy-start.78 = (s32[128]{0:T(128)S(1)}, s32[128]{0:T(128)}, u32[]{:S(2)}) copy-start(s32[128]{0:T(128)} %param.27) | copy-start | bytes 1540
  8.6 249.8 %copy-start.62 = (f32[1024]{0:T(1024)S(1)}, f32[1024]{0:T(1024)}, u32[]{:S(2)}) copy-start(f32[1024]{0:T(1024)} %param.16) | copy-start | bytes 12292
  258.6 8.4 %copy-start.8 = (bf16[128,1024]{1,0:T(8,128)(2,1)}, bf16[128,1024]{1,0:T(8,128)(2,1)S(1)}, u32[]{:S(2)}) copy-start(bf16[128,1024]{1,0:T(8,128)(2,1)S(1)} %fusion.18) | copy-start | bytes 786436
  288.6 7.1 copy-start.34
  288.6 7.1 copy-start.60
  288.6 7.1 copy-start.73
  296.6 107.7 %all-gather.10.cloned.1.call-start = ((), (), s32[]{:S(2)}) async-start(), calls=%async_computation.5 | async-start | bytes 3932160 | tf_op jit(solution)/shard_map/all_gather | solution.py:487
  297.3 171.1 %all-gather.12.cloned.1.call-start = ((), (), s32[]{:S(2)}) async-start(), calls=%async_computation.6 | async-start | bytes 3932160 | tf_op jit(solution)/shard_map/all_gather | solution.py:487
  303.0 251.4 %all-gather.20.cloned.1.call-start = ((), (), s32[]{:S(2)}) async-start(), calls=%async_computation.10 | async-start | bytes 1310720 | tf_op jit(solution)/shard_map/all_gather | solution.py:490
  336.0 5.7 copy-start.58
  337.4 7.2 copy-start.2
  353.7 119.6 %copy-start.27 = (bf16[128,3072]{1,0:T(8,128)(2,1)S(1)}, bf16[128,3072]{1,0:T(8,128)(2,1)}, u32[]{:S(2)}) copy-start(bf16[128,3072]{1,0:T(8,128)(2,1)} %get-tuple-element.76) | copy-start | bytes 2359300
  468.5 88.4 %all-gather.18.cloned.1.call-start = ((), (), s32[]{:S(2)}) async-start(), calls=%async_computation.9 | async-start | bytes 1310720 | tf_op jit(solution)/shard_map/all_gather | solution.py:490
  469.8 24.1 %copy-start.16 = (bf16[8,128,2,128]{3,1,2,0:T(8,128)(2,1)S(1)}, bf16[8,128,2,128]{3,1,2,0:T(8,128)(2,1)}, u32[]{:S(2)}) copy-start(bf16[8,128,2,128]{3,1,2,0:T(8,128)(2,1)} %copy-done.15) | copy-start | bytes 1572868
  469.8 17.6 %all-to-all-start.2 = ((bf16[128,4,256]{2,0,1:T(8,128)(2,1)}), bf16[128,4,256]{2,0,1:T(8,128)(2,1)S(1)}, u32[]{:S(2)}, u32[]{:S(2)}) async-start(bf16[128,4,256]{2,0,1:T(8,128)(2,1)} %bitcast.217), calls=%async_computation.2 | async-start | bytes 524288 | tf_op jit(solution)/shard_map/all_to_all | solution.py:483
  487.3 32.4 %copy-start.9 = (bf16[128,1024]{1,0:T(8,128)(2,1)S(1)}, bf16[128,1024]{1,0:T(8,128)(2,1)}, u32[]{:S(2)}) copy-start(bf16[128,1024]{1,0:T(8,128)(2,1)} %copy-done.8) | copy-start | bytes 786436
  487.3 33.1 %copy-start.82 = (bf16[512,1024]{1,0:T(8,128)(2,1)S(1)}, bf16[512,1024]{1,0:T(8,128)(2,1)}, u32[]{:S(2)}) copy-start(bf16[512,1024]{1,0:T(8,128)(2,1)} %all-gather.8.cloned.1.call-done) | copy-start | bytes 3145732
  487.3 28.7 %all-to-all-start.3 = ((bf16[128,4,768]{2,0,1:T(8,128)(2,1)}), bf16[128,4,768]{2,0,1:T(8,128)(2,1)S(1)}, u32[]{:S(2)}, u32[]{:S(2)}) async-start(bf16[128,4,768]{2,0,1:T(8,128)(2,1)} %bitcast.216), calls=%async_computation.3 | async-start | bytes 1572864 | tf_op jit(solution)/shard_map/all_to_all | solution.py:484
  493.1 106.2 %all-gather.16.cloned.1.call-start = ((), (), s32[]{:S(2)}) async-start(), calls=%async_computation.8 | async-start | bytes 2621440 | tf_op jit(solution)/shard_map/all_gather | solution.py:490
  516.0 28.2 %all-to-all-start.1 = ((bf16[128,4,512]{2,0,1:T(8,128)(2,1)}), bf16[128,4,512]{2,0,1:T(8,128)(2,1)S(1)}, u32[]{:S(2)}, u32[]{:S(2)}) async-start(bf16[128,4,512]{2,0,1:T(8,128)(2,1)} %copy.188), calls=%async_computation.1 | async-start | bytes 1048576 | tf_op jit(solution)/shard_map/all_to_all | solution.py:482
  522.6 25.1 %copy-start.83 = (bf16[512,1024]{1,0:T(8,128)(2,1)S(1)}, bf16[512,1024]{1,0:T(8,128)(2,1)}, u32[]{:S(2)}) copy-start(bf16[512,1024]{1,0:T(8,128)(2,1)} %all-gather.14.cloned.1.call-done) | copy-start | bytes 3145732
  544.2 10.2 %all-to-all-start = ((bf16[128,4,256]{2,0,1:T(8,128)(2,1)}), bf16[128,4,256]{2,0,1:T(8,128)(2,1)S(1)}, u32[]{:S(2)}, u32[]{:S(2)}) async-start(bf16[128,4,256]{2,0,1:T(8,128)(2,1)} %bitcast.218), calls=%async_computation | async-start | bytes 524288 | tf_op jit(solution)/shard_map/all_to_all | solution.py:481
  547.6 178.3 %all-reduce.4.cloned.1.call-start = ((), (), s32[]{:S(2)}) async-start(), calls=%async_computation.11 | async-start | bytes 15728640 | tf_op jit(solution)/shard_map/psum | solution.py:506
  607.4 41.7 %copy-start.22 = (f32[128,1024]{1,0:T(8,128)S(1)}, f32[128,1024]{1,0:T(8,128)}, u32[]{:S(2)}) copy-start(f32[128,1024]{1,0:T(8,128)} %copy-done.21) | copy-start | bytes 1572868
  607.4 41.7 %copy-start.35 = (bf16[128,1024]{1,0:T(8,128)(2,1)S(1)}, bf16[128,1024]{1,0:T(8,128)(2,1)}, u32[]{:S(2)}) copy-start(bf16[128,1024]{1,0:T(8,128)(2,1)} %param.29) | copy-start | bytes 786436
  607.5 41.7 %copy-start.61 = (f32[1024]{0:T(1024)S(1)}, f32[1024]{0:T(1024)}, u32[]{:S(2)}) copy-start(f32[1024]{0:T(1024)} %param.23) | copy-start | bytes 12292
  607.5 41.7 %copy-start.74 = (f32[128]{0:T(128)S(1)}, f32[128]{0:T(128)}, u32[]{:S(2)}) copy-start(f32[128]{0:T(128)} %copy-done.72) | copy-start | bytes 1540
  607.5 41.7 %copy-start.80 = (f32[128]{0:T(128)S(1)}, f32[128]{0:T(128)}, u32[]{:S(2)}) copy-start(f32[128]{0:T(128)} %copy-done.79) | copy-start | bytes 1540
  609.2 41.0 %copy-start.28 = (bf16[128,3072]{1,0:T(8,128)(2,1)S(1)}, bf16[128,3072]{1,0:T(8,128)(2,1)}, u32[]{:S(2)}) copy-start(bf16[128,3072]{1,0:T(8,128)(2,1)} %get-tuple-element.76) | copy-start | bytes 2359300
  (70 other events, 154.8 us)
Sparse Core Ops, SparseCore 0:
  9.6 59.1 all-gather.7
  296.7 43.1 all-gather.13
  341.5 62.8 all-gather.9
  406.3 62.0 all-gather.11
  470.4 40.5 all-gather.19
  512.4 40.0 all-gather.17
  554.6 44.6 all-gather.15
  604.7 121.2 all-reduce.3
